TPU v7x, 32 devices: a whole 2x2x4 slice. The times are simulated.
32 devices in a mesh: seq: 2 (over x), ctx: 16 (over z, y, core).
Axes of the slice: x: 2, y: 2, z: 4, core: 2. Of those that a mesh axis runs over, the one named last changes fastest.
Arguments:
- inputs: bfloat16 [2, 2048, 768], P('seq', 'ctx'), may hold values from -6 to 6
- lengths: int32 [2], P('seq'), may hold values from 512 to 2048, as said below
- cotangent: bfloat16 [2, 2048, 768], P('seq', 'ctx'), may hold values from -6 to 6
- w_qkv: bfloat16 [768, 2304], P(('seq', 'ctx')), may hold values from -0.21875 to 0.21875
- w_out: bfloat16 [768, 768], P(('seq', 'ctx')), may hold values from -6 to 6
- w_in: bfloat16 [768, 3072], P(('seq', 'ctx')), may hold values from -0.21875 to 0.21875
- w_back: bfloat16 [3072, 768], P(('seq', 'ctx')), may hold values from -0.109375 to 0.109375
- vectors: bfloat16 [768, 8], P(('seq', 'ctx')), may hold values from -1 to 2
- ffn_bias: bfloat16 [3072], P(('seq', 'ctx')), may hold values from -2 to 2
Outputs:
- result: bfloat16 [2, 2048, 768], P('seq', 'ctx')
- grad_inputs: float32 [2, 2048, 768], P('seq', 'ctx')
- grad_w_qkv: float32 [768, 2304], P(('seq', 'ctx'))
- grad_w_out: float32 [768, 768], P(('seq', 'ctx'))
- grad_w_in: float32 [768, 3072], P(('seq', 'ctx'))
- grad_w_back: float32 [3072, 768], P(('seq', 'ctx'))
- grad_vectors: float32 [768, 8], P(('seq', 'ctx'))
- grad_ffn_bias: float32 [3072], P(('seq', 'ctx'))
Inputs may be any that keep to these rules, and one draw needn't show every extreme that they name: `lengths`: one sequence of each draw is full.
All inputs are finite; a program needn't handle non-finite values.
Results may differ from a plain program's by a relative error of at most 0.025.
Values may be sent and summed in bfloat16 or wider, within the bound.
A program may use at most 448 MiB of HBM per device.

v0:
```python
import jax
import jax.numpy as jnp
from jax import lax
from jax.sharding import PartitionSpec as P

HEADS = 12


EPSILON = 1e-12
MASKED = -1e30


def layer_norm(values_in, norm_gain, norm_shift):
    average = jnp.mean(values_in, axis=-1, keepdims=True)
    centred = values_in - average
    spread = jnp.mean(centred * centred, axis=-1, keepdims=True)
    return centred * lax.rsqrt(spread + EPSILON) * norm_gain + norm_shift


def gelu_exact(values_in):
    return jax.nn.gelu(values_in, approximate=False)


def key_spans(extent_all):
    number_parts = min(8, max(1, -(-extent_all // 2048)))
    span_size = -(-extent_all // number_parts)
    return [
        (offset, min(span_size, extent_all - offset)) for offset in range(0, extent_all, span_size)
    ]


def to_heads(row_block, head_count):
    row_total = row_block.shape[0]
    return row_block.reshape(row_total, head_count, -1).transpose(1, 0, 2)


def online_merge(running, query_heads, key_block, value_block, key_start, length, score_scale):
    top_old, total_old, accum_old = running
    head_count = query_heads.shape[0]
    key_width = key_block.shape[0]
    key_heads = key_block.reshape(key_width, head_count, -1)
    value_heads = value_block.reshape(key_width, head_count, -1)
    scores = (
        jnp.einsum("hqd,khd->hqk", query_heads, key_heads, preferred_element_type=jnp.float32)
        * score_scale
    )
    usable = (key_start + jnp.arange(key_width, dtype=jnp.int32) < length)[None, None, :]
    masked = jnp.where(usable, scores, MASKED)
    top_new = jnp.maximum(top_old, jnp.max(masked, axis=-1))
    factor = jnp.exp(top_old - top_new)
    weights_here = jnp.where(usable, jnp.exp(masked - top_new[:, :, None]), 0.0)
    total_new = total_old * factor + jnp.sum(weights_here, axis=-1)
    accum_new = accum_old * factor[:, :, None] + jnp.einsum(
        "hqk,khd->hqd",
        weights_here.astype(jnp.bfloat16),
        value_heads,
        preferred_element_type=jnp.float32,
    )
    return (top_new, total_new, accum_new)


def score_grads(
    query_heads,
    grad_heads,
    log_total,
    row_delta,
    key_block,
    value_block,
    key_start,
    length,
    score_scale,
):
    head_count = query_heads.shape[0]
    key_width = key_block.shape[0]
    key_heads = key_block.reshape(key_width, head_count, -1)
    value_heads = value_block.reshape(key_width, head_count, -1)
    scores = (
        jnp.einsum("hqd,khd->hqk", query_heads, key_heads, preferred_element_type=jnp.float32)
        * score_scale
    )
    usable = (key_start + jnp.arange(key_width, dtype=jnp.int32) < length)[None, None, :]
    soft_weights = jnp.where(usable, jnp.exp(scores - log_total[:, :, None]), 0.0)
    grad_soft = jnp.einsum(
        "hqd,khd->hqk", grad_heads, value_heads, preferred_element_type=jnp.float32
    )
    grad_scores = (soft_weights * (grad_soft - row_delta[:, :, None])).astype(jnp.bfloat16)
    return (key_heads, grad_scores, soft_weights.astype(jnp.bfloat16))


def per_device(inputs, lengths, cotangent, w_qkv, w_out, w_in, w_back, vectors, ffn_bias):
    own_rows = inputs[0]
    row_count = own_rows.shape[0]
    model_width = own_rows.shape[1]
    head_count = HEADS
    head_size = model_width // head_count
    score_scale = head_size ** (-0.5)
    length = lengths[0]
    ctx_size = lax.axis_size("ctx")
    row_start = lax.axis_index("ctx") * row_count
    qkv_full, vector_full = (
        lax.all_gather(w_qkv, ("seq", "ctx"), axis=0, tiled=True),
        lax.all_gather(vectors, ("seq", "ctx"), axis=0, tiled=True),
    )
    vec = vector_full.astype(jnp.float32)
    projected = jnp.dot(own_rows, qkv_full, preferred_element_type=jnp.float32)
    query_rows = (projected[:, :model_width] + vec[:, 0]).astype(jnp.bfloat16)
    key_rows = projected[:, model_width : 2 * model_width].astype(jnp.bfloat16)
    value_rows = (projected[:, 2 * model_width :] + vec[:, 1]).astype(jnp.bfloat16)
    query_heads = to_heads(query_rows, head_count)
    start_state = (
        jnp.full((head_count, row_count), MASKED, jnp.float32),
        jnp.zeros((head_count, row_count), jnp.float32),
        jnp.zeros((head_count, row_count, head_size), jnp.float32),
    )
    running = start_state
    piece_start = jnp.int32(0)
    key_piece = lax.all_gather(key_rows, "ctx", axis=0, tiled=True)
    value_piece = lax.all_gather(value_rows, "ctx", axis=0, tiled=True)
    for offset, extent in key_spans(key_piece.shape[0]):
        running = online_merge(
            running,
            query_heads,
            key_piece[offset : offset + extent],
            value_piece[offset : offset + extent],
            piece_start + offset,
            length,
            score_scale,
        )
    row_top, row_total, accum = running
    out_full, in_full, back_full, ffn_full = (
        lax.all_gather(w_out, ("seq", "ctx"), axis=0, tiled=True),
        lax.all_gather(w_in, ("seq", "ctx"), axis=0, tiled=True),
        lax.all_gather(w_back, ("seq", "ctx"), axis=0, tiled=True),
        lax.all_gather(ffn_bias, ("seq", "ctx"), axis=0, tiled=True),
    )
    attended_f = accum / row_total[:, :, None]
    log_total = row_top + jnp.log(row_total)
    attended = attended_f.transpose(1, 0, 2).reshape(row_count, model_width).astype(jnp.bfloat16)
    branch = jnp.dot(attended, out_full, preferred_element_type=jnp.float32) + vec[:, 2]
    first_in = own_rows.astype(jnp.float32) + branch
    normed_first, first_back = jax.vjp(layer_norm, first_in, vec[:, 3], vec[:, 4])
    first_low = normed_first.astype(jnp.bfloat16)
    hidden = jnp.dot(first_low, in_full, preferred_element_type=jnp.float32) + ffn_full.astype(
        jnp.float32
    )
    active_f, gelu_back = jax.vjp(gelu_exact, hidden)
    active = active_f.astype(jnp.bfloat16)
    second = jnp.dot(active, back_full, preferred_element_type=jnp.float32) + vec[:, 5]
    result, second_back = jax.vjp(layer_norm, normed_first + second, vec[:, 6], vec[:, 7])
    valid_rows = (row_start + jnp.arange(row_count, dtype=jnp.int32) < length).astype(jnp.float32)[
        :, None
    ]
    grad_result = cotangent[0].astype(jnp.float32) * valid_rows
    grad_second, grad_gain_two, grad_shift_two = second_back(grad_result)
    grad_second_low = grad_second.astype(jnp.bfloat16)
    grad_active = jnp.dot(grad_second_low, back_full.T, preferred_element_type=jnp.float32)
    grad_w_back = jnp.dot(active.T, grad_second_low, preferred_element_type=jnp.float32)
    grad_hidden = gelu_back(grad_active)[0].astype(jnp.bfloat16)
    grad_w_in = jnp.dot(first_low.T, grad_hidden, preferred_element_type=jnp.float32)
    grad_first = grad_second + jnp.dot(grad_hidden, in_full.T, preferred_element_type=jnp.float32)
    grad_branch_full, grad_gain_one, grad_shift_one = first_back(grad_first)
    grad_branch = grad_branch_full.astype(jnp.bfloat16)
    grad_w_out = jnp.dot(attended.T, grad_branch, preferred_element_type=jnp.float32)
    grad_attended = jnp.dot(grad_branch, out_full.T, preferred_element_type=jnp.float32).astype(
        jnp.bfloat16
    )
    grad_heads = to_heads(grad_attended, head_count)
    row_delta = jnp.sum(grad_heads.astype(jnp.float32) * attended_f, axis=-1)
    zero_query = jnp.zeros((head_count, row_count, head_size), jnp.float32)
    key_all, value_all = (
        lax.all_gather(key_rows, "ctx", axis=0, tiled=True),
        lax.all_gather(value_rows, "ctx", axis=0, tiled=True),
    )
    group_size = 1
    while group_size * 2 * row_count <= 2048 and ctx_size % (group_size * 2) == 0:
        group_size = group_size * 2
    block_rows = group_size * row_count
    blocks_total = ctx_size // group_size

    def grad_step(grad_query, block_in):
        key_block, value_block, block_start = block_in
        key_heads, grad_scores, soft_low = score_grads(
            query_heads,
            grad_heads,
            log_total,
            row_delta,
            key_block,
            value_block,
            block_start,
            length,
            score_scale,
        )
        grad_query = (
            grad_query
            + jnp.einsum("hqk,khd->hqd", grad_scores, key_heads, preferred_element_type=jnp.float32)
            * score_scale
        )
        grad_key = (
            jnp.einsum("hqk,hqd->khd", grad_scores, query_heads, preferred_element_type=jnp.float32)
            * score_scale
        )
        grad_value = jnp.einsum(
            "hqk,hqd->khd", soft_low, grad_heads, preferred_element_type=jnp.float32
        )
        joined = jnp.concatenate(
            (
                grad_key.reshape(block_rows, model_width),
                grad_value.reshape(block_rows, model_width),
            ),
            axis=1,
        )
        return (grad_query, joined)

    block_starts = jnp.arange(blocks_total, dtype=jnp.int32) * block_rows
    grad_query, grad_terms = lax.scan(
        grad_step,
        zero_query,
        (
            key_all.reshape(blocks_total, block_rows, model_width),
            value_all.reshape(blocks_total, block_rows, model_width),
            block_starts,
        ),
    )
    owned = lax.psum_scatter(
        grad_terms.reshape(blocks_total * block_rows, 2 * model_width),
        "ctx",
        scatter_dimension=0,
        tiled=True,
    )
    grad_key_rows = owned[:, :model_width]
    grad_value_rows = owned[:, model_width:]
    grad_query_low = (
        grad_query.transpose(1, 0, 2).reshape(row_count, model_width).astype(jnp.bfloat16)
    )
    grad_key_low = grad_key_rows.astype(jnp.bfloat16)
    grad_value_low = grad_value_rows.astype(jnp.bfloat16)
    grad_projected = jnp.concatenate((grad_query_low, grad_key_low, grad_value_low), axis=1)
    grad_w_qkv = jnp.dot(own_rows.T, grad_projected, preferred_element_type=jnp.float32)
    grad_inputs = grad_branch_full + jnp.dot(
        grad_projected, qkv_full.T, preferred_element_type=jnp.float32
    )
    grad_vectors = jnp.stack(
        (
            jnp.sum(grad_query_low.astype(jnp.float32), axis=0),
            jnp.sum(grad_value_low.astype(jnp.float32), axis=0),
            jnp.sum(grad_branch.astype(jnp.float32), axis=0),
            grad_gain_one,
            grad_shift_one,
            jnp.sum(grad_second_low.astype(jnp.float32), axis=0),
            grad_gain_two,
            grad_shift_two,
        ),
        axis=1,
    )
    grad_ffn = jnp.sum(grad_hidden.astype(jnp.float32), axis=0)
    summed_grads = (
        lax.psum_scatter(grad_w_qkv, ("seq", "ctx"), scatter_dimension=0, tiled=True),
        lax.psum_scatter(grad_w_out, ("seq", "ctx"), scatter_dimension=0, tiled=True),
        lax.psum_scatter(grad_w_in, ("seq", "ctx"), scatter_dimension=0, tiled=True),
        lax.psum_scatter(grad_w_back, ("seq", "ctx"), scatter_dimension=0, tiled=True),
        lax.psum_scatter(grad_vectors, ("seq", "ctx"), scatter_dimension=0, tiled=True),
        lax.psum_scatter(grad_ffn, ("seq", "ctx"), scatter_dimension=0, tiled=True),
    )
    return (
        result.astype(jnp.bfloat16)[None],
        grad_inputs[None],
        summed_grads[0],
        summed_grads[1],
        summed_grads[2],
        summed_grads[3],
        summed_grads[4],
        summed_grads[5],
    )


def solution(mesh):
    return jax.shard_map(
        per_device,
        mesh=mesh,
        in_specs=(
            P("seq", "ctx", None),
            P("seq"),
            P("seq", "ctx", None),
            P(("seq", "ctx"), None),
            P(("seq", "ctx"), None),
            P(("seq", "ctx"), None),
            P(("seq", "ctx"), None),
            P(("seq", "ctx"), None),
            P(("seq", "ctx")),
        ),
        out_specs=(
            P("seq", "ctx", None),
            P("seq", "ctx", None),
            P(("seq", "ctx"), None),
            P(("seq", "ctx"), None),
            P(("seq", "ctx"), None),
            P(("seq", "ctx"), None),
            P(("seq", "ctx"), None),
            P(("seq", "ctx")),
        ),
        check_vma=False,
    )
```

profile of v0, /device:TPU:0, one launch (start us, length us, event | category | flops | bytes accessed | tf_op | source)
XLA Modules:
  0.0 1052.9 jit_solution(521782439624674951)
XLA Ops:
  7.9 43.8 %all-gather = bf16[32,24,8]{1,2,0:T(8,128)(2,1)S(1)} all-gather(bf16[1,24,8]{1,2,0:T(8,128)(2,1)} %bitcast.104), channel_id=1, replica_groups=mesh['seq'=2,'ctx'=16] {'seq','ctx'}, dimensions={0}, use_global_device_ids=true | all-gather | bytes 12672 | tf_op jit(solution)/shard_map/all_gather | solution.py:102
  52.1 21.5 %all-gather.8.cloned.1.call-done = bf16[768,2304]{1,0:T(8,128)(2,1)} async-done(((bf16[24,2304]{1,0:T(8,128)(2,1)}), bf16[768,2304]{1,0:T(8,128)(2,1)}) %all-gather.8.cloned.1.call-update) | async-done | bytes 3538960 | tf_op jit(solution)/shard_map/all_gather | solution.py:101
  73.6 2.8 fusion.36
  80.7 39.0 %all-reduce = bf16[3072]{0:T(1024)(128)(2,1)S(1)} all-reduce(bf16[3072]{0:T(1024)(128)(2,1)S(1)} %dynamic-update-slice), channel_id=1, replica_groups=mesh['seq'=2,'ctx'=16] {'seq','ctx'}, use_global_device_ids=true, to_apply=%add | all-reduce | flops 3072 | bytes 12288
  121.6 4.7 copy.40
  126.3 42.0 %all-gather.10.cloned.1.call-done = bf16[2048,768]{1,0:T(8,128)(2,1)} async-done(((bf16[128,768]{1,0:T(8,128)(2,1)}), bf16[2048,768]{1,0:T(8,128)(2,1)}) %all-gather.10.cloned.1.call-update) | async-done | bytes 3145744 | tf_op jit(solution)/shard_map/all_gather | solution.py:117
  168.2 4.7 copy.39
  173.0 3.9 select_reduce_fusion
  176.9 3.2 fusion.1
  181.4 5.6 fusion.32
  187.0 36.4 %all-gather.14.cloned.1.call-done = bf16[768,768]{1,0:T(8,128)(2,1)} async-done(((bf16[24,768]{1,0:T(8,128)(2,1)}), bf16[768,768]{1,0:T(8,128)(2,1)}) %all-gather.14.cloned.1.call-update) | async-done | bytes 1179664 | tf_op jit(solution)/shard_map/all_gather | solution.py:131
  225.5 63.2 %all-gather.16.cloned.1.call-done = bf16[768,3072]{1,0:T(8,128)(2,1)} async-done(((bf16[24,3072]{1,0:T(8,128)(2,1)}), bf16[768,3072]{1,0:T(8,128)(2,1)}) %all-gather.16.cloned.1.call-update) | async-done | bytes 4718608 | tf_op jit(solution)/shard_map/all_gather | solution.py:132
  288.7 8.4 multiply_convert_fusion.1
  297.1 56.3 %all-gather.18.cloned.1.call-done = bf16[3072,768]{1,0:T(8,128)(2,1)} async-done(((bf16[96,768]{1,0:T(8,128)(2,1)}), bf16[3072,768]{1,0:T(8,128)(2,1)}) %all-gather.18.cloned.1.call-update) | async-done | bytes 4718608 | tf_op jit(solution)/shard_map/all_gather | solution.py:133
  353.4 3.4 fusion.56
  358.9 2.5 convert_reduce_fusion
  366.2 9.9 fusion.3
  376.3 7.3 multiply_convert_fusion
  383.6 4.1 convolution_multiply_fusion
  388.2 11.4 %pad_maximum_fusion = f32[2048,1536]{0,1:T(8,128)} fusion(f32[2048,768]{0,1:T(8,128)} %bitcast.88, f32[2048,768]{0,1:T(8,128)} %bitcast.85), kind=kLoop, calls=%fused_computation | loop fusion | flops 3145728 | bytes 25165824 | tf_op jit(solution)/shard_map/while/body/eval_jaxpr/concatenate | solution.py:205
  402.7 6.1 fusion.49
  408.9 6.0 fusion.58
  417.3 6.6 convert_reduce_fusion.4
  423.8 108.9 %reduce-scatter.9.cloned.1.call-done = f32[128,1536]{0,1:T(8,128)} async-done(((f32[2048,1536]{0,1:T(8,128)}), f32[128,1536]{0,1:T(8,128)}) %reduce-scatter.9.cloned.1.call-update) | async-done | bytes 786448 | tf_op jit(solution)/shard_map/reduce_scatter | solution.py:224
  534.7 5.0 convolution_bitcast_fusion
  539.6 8.0 copy.43
  556.2 40.7 %all-reduce.3 = (f32[768,8]{0,1:T(8,128)}, f32[3072]{0:T(1024)S(1)}) all-reduce(f32[768,8]{0,1:T(8,128)} %stack.35, f32[3072]{0:T(1024)} %get-tuple-element.86), channel_id=7, replica_groups=mesh['seq'=2,'ctx'=16] {'seq','ctx'}, use_global_device_ids=true, to_apply=%region_24.25.clone | all-reduce | flops 9216 | bytes 73728
  598.9 3.3 fusion.19
  602.1 35.7 %reduce-scatter.11.cloned.1.call-done = f32[24,768]{1,0:T(8,128)} async-done(((f32[768,768]{1,0:T(8,128)}), f32[24,768]{1,0:T(8,128)}) %reduce-scatter.11.cloned.1.call-update) | async-done | bytes 73744 | tf_op jit(solution)/shard_map/reduce_scatter | solution.py:258
  637.8 142.0 %reduce-scatter.13.cloned.1.call-done = f32[24,3072]{1,0:T(8,128)} async-done(((f32[768,3072]{1,0:T(8,128)}), f32[24,3072]{1,0:T(8,128)}) %reduce-scatter.13.cloned.1.call-update) | async-done | bytes 294928 | tf_op jit(solution)/shard_map/reduce_scatter | solution.py:259
  779.8 141.8 %reduce-scatter.15.cloned.1.call-done = f32[96,768]{1,0:T(8,128)} async-done(((f32[3072,768]{1,0:T(8,128)}), f32[96,768]{1,0:T(8,128)}) %reduce-scatter.15.cloned.1.call-update) | async-done | bytes 294928 | tf_op jit(solution)/shard_map/reduce_scatter | solution.py:260
  921.6 124.7 %reduce-scatter.17.cloned.1.call-done = f32[24,2304]{1,0:T(8,128)} async-done(((f32[768,2304]{1,0:T(8,128)}), f32[24,2304]{1,0:T(8,128)}) %reduce-scatter.17.cloned.1.call-update) | async-done | bytes 221200
  (116 shorter events, 35.3 us)
Async XLA Ops:
  7.2 66.5 %all-gather.8.cloned.1.call-start = ((), (), s32[]{:S(2)}) async-start(), calls=%async_computation.5 | async-start | bytes 3649536 | tf_op jit(solution)/shard_map/all_gather | solution.py:101
  7.9 113.7 %all-gather.12.cloned.1.call-start = ((), (), s32[]{:S(2)}) async-start(), calls=%async_computation.7 | async-start | bytes 3342336 | tf_op jit(solution)/shard_map/all_gather | solution.py:118
  76.4 4.0 copy-start.14
  77.2 91.1 %all-gather.10.cloned.1.call-start = ((), (), s32[]{:S(2)}) async-start(), calls=%async_computation.6 | async-start | bytes 3342336 | tf_op jit(solution)/shard_map/all_gather | solution.py:117
  77.9 145.5 %all-gather.14.cloned.1.call-start = ((), (), s32[]{:S(2)}) async-start(), calls=%async_computation.8 | async-start | bytes 1216512 | tf_op jit(solution)/shard_map/all_gather | solution.py:131
  78.5 210.2 %all-gather.16.cloned.1.call-start = ((), (), s32[]{:S(2)}) async-start(), calls=%async_computation.9 | async-start | bytes 4866048 | tf_op jit(solution)/shard_map/all_gather | solution.py:132
  79.1 274.3 %all-gather.18.cloned.1.call-start = ((), (), s32[]{:S(2)}) async-start(), calls=%async_computation.10 | async-start | bytes 4866048 | tf_op jit(solution)/shard_map/all_gather | solution.py:133
  79.7 453.1 %reduce-scatter.9.cloned.1.call-start = ((), (), s32[]{:S(2)}) async-start(), calls=%async_computation.11 | async-start | bytes 13369344 | tf_op jit(solution)/shard_map/reduce_scatter | solution.py:224
  176.9 4.6 copy-start
  181.4 42.0 %copy-start.8 = (bf16[1,128,768]{2,1,0:T(8,128)(2,1)S(1)}, bf16[1,128,768]{2,1,0:T(8,128)(2,1)}, u32[]{:S(2)}) copy-start(bf16[1,128,768]{2,1,0:T(8,128)(2,1)} %param.9) | copy-start | bytes 589828
  353.4 5.5 slice-start
  353.4 3.6 copy-start.9
  353.4 3.6 copy-start.12
  353.4 5.5 slice-start.1
  353.4 5.5 copy-start.16
  356.8 2.2 copy-start.15
  358.2 3.2 slice-start.2
  358.9 2.5 slice-start.3
  363.8 1.7 copy-start.5
  364.0 0.8 copy-start.6
  364.1 12.1 %copy-start.13 = (f32[128]{0:T(128)}, f32[128]{0:T(128)S(1)}, u32[]{:S(2)}) copy-start(f32[128]{0:T(128)S(1)} %negate_multiply_fusion.1) | copy-start | bytes 1540
  366.2 9.9 copy-start.11
  366.2 10.0 copy-start.7
  383.6 4.6 copy-start.1
  399.5 0.9 copy-start.10
  399.6 238.3 %reduce-scatter.11.cloned.1.call-start = ((), (), s32[]{:S(2)}) async-start(), calls=%async_computation.12 | async-start | bytes 2433024 | tf_op jit(solution)/shard_map/reduce_scatter | solution.py:258
  402.4 377.4 %reduce-scatter.13.cloned.1.call-start = ((), (), s32[]{:S(2)}) async-start(), calls=%async_computation.13 | async-start | bytes 9732096 | tf_op jit(solution)/shard_map/reduce_scatter | solution.py:259
  408.8 512.8 %reduce-scatter.15.cloned.1.call-start = ((), (), s32[]{:S(2)}) async-start(), calls=%async_computation.14 | async-start | bytes 9732096 | tf_op jit(solution)/shard_map/reduce_scatter | solution.py:260
  414.9 2.4 copy-start.2
  414.9 631.4 %reduce-scatter.17.cloned.1.call-start = ((), (), s32[]{:S(2)}) async-start(), calls=%async_computation.15 | async-start | bytes 7299072
  533.9 0.7 copy-start.4
  547.7 51.2 %copy-start.3 = (bf16[768,2304]{1,0:T(8,128)(2,1)S(1)}, bf16[768,2304]{1,0:T(8,128)(2,1)}, u32[]{:S(2)}) copy-start(bf16[768,2304]{1,0:T(8,128)(2,1)} %all-gather.8.cloned.1.call-done) | copy-start | bytes 10616836
Sparse Core Ops, SparseCore 0:
  10.9 62.7 all-gather.7
  77.3 44.2 all-gather.11
  124.4 43.7 all-gather.9
  171.0 52.3 all-gather.13
  226.2 62.4 all-gather.15
  291.4 61.8 all-gather.17
  399.7 133.0 reduce-scatter.8
  538.6 99.1 reduce-scatter.10
  644.3 135.4 reduce-scatter.12
  786.1 135.4 reduce-scatter.14
  927.9 118.3 reduce-scatter.16
where the time goes:
time: 1050 us
  waiting for transfers between devices  776 us (74%)
  blocking collectives  123 us (12%)
  matrix products  81.4 us (8%)
  local copies, waits for them, and re-layouts  35 us (3%)
  other arithmetic  21.5 us (2%)
  between operations  14.8 us (1%)
    reduce_scatter x1, waiting for transfers between devices, per_device(): lax.psum_scatter(grad_w_in, ('seq', 'ctx'), scatter_dimension=0, tiled=True)  142 us
    reduce_scatter x1, waiting for transfers between devices, per_device(): lax.psum_scatter(grad_w_back, ('seq', 'ctx'), scatter_dimension=0, tiled=...  142 us
    unnamed x12, waiting for transfers between devices  127 us
    reduce_scatter x1, waiting for transfers between devices, per_device(): lax.psum_scatter(grad_terms.reshape(blocks_total * block_rows, 2 * model_...  109 us
    unnamed x2, blocking collectives  79.7 us
    all_gather x1, waiting for transfers between devices, per_device(): lax.all_gather(w_in, ('seq', 'ctx'), axis=0, tiled=True)  63.2 us
    all_gather x1, waiting for transfers between devices, per_device(): lax.all_gather(w_back, ('seq', 'ctx'), axis=0, tiled=True)  56.3 us
    all_gather x1, blocking collectives, per_device(): lax.all_gather(vectors, ('seq', 'ctx'), axis=0, tiled=True)  43.8 us
  transfers between devices with their start and end apart: 11, of which 11 were waited for; matrix products, arithmetic and copies ran while one was open for 8% of the time, Pallas kernels for 0%

commit v1 on v0

v1 whole, which is shorter than its diff:
```python
import functools, math
import jax, jax.numpy as jnp
from jax import lax
from jax.experimental import pallas as pl
from jax.experimental.pallas import tpu as pltpu

MESH = pl.DeviceIdType.MESH

class Grid:
    def __init__(self, seqs, ctx):
        self.seqs, self.ctx = seqs, ctx
        self.depth = ctx // 4
    def here(self):
        s, i = lax.axis_index("seq"), lax.axis_index("ctx")
        return s, i // 4, (i // 2) % 2, i % 2

def cid(z, y, c):
    return (z * 2 + y) * 2 + c

def greet(grid, with_seq):
    s, z, y, c = grid.here()
    bar = pltpu.get_barrier_semaphore()
    def hello(p):
        pl.semaphore_signal(bar, inc=1, device_id=p, device_id_type=MESH)
    peers = [(s, cid(z, 1 - y, c)), (s, cid(z, y, 1 - c))]
    if with_seq:
        peers += [(1 - s, cid(z, y, c))]
    for p in peers:
        hello(p)
    @pl.when(z > 0)
    def _():
        hello((s, cid(z - 1, y, c)))
    @pl.when(z < grid.depth - 1)
    def _():
        hello((s, cid(z + 1, y, c)))
    ends = jnp.where(z > 0, 1, 0) + jnp.where(z < grid.depth - 1, 1, 0)
    pl.semaphore_wait(bar, len(peers) + ends)

def each(n, body):
    if n <= 4:
        for k in range(n):
            body(k)
    else:
        lax.fori_loop(0, n, lambda k, _: (body(k), None)[1], None)

class Gather:
    def __init__(self, grid, src, dst, send, zsend, recv, local, order, cols=None):
        self.g, self.src, self.dst = grid, src, dst
        self.send, self.zsend, self.recv, self.local, self.order = send, zsend, recv, local, order
        self.cols = cols
        self.s, self.z, self.y, self.c = grid.here()
        self.rest = order[1:]
    def view(self, b):
        return self.dst.at[b] if self.cols is None else self.dst.at[b, :, self.cols]
    def own(self):
        return self.src.at[0] if self.cols is None else self.src.at[0, :, self.cols]
    def push(self, src, b, dev, sem):
        pltpu.make_async_remote_copy(src, self.view(b), sem, self.recv.at[b], device_id=dev, device_id_type=MESH).start()
    def wait(self, b, sem=None):
        v = self.view(b)
        pltpu.make_async_copy(v, v, self.recv.at[b] if sem is None else sem).wait()
    def dev(self, dim):
        if dim == 'x': return (1 - self.s, cid(self.z, self.y, self.c))
        if dim == 'y': return (self.s, cid(self.z, 1 - self.y, self.c))
        if dim == 'c': return (self.s, cid(self.z, self.y, 1 - self.c))
        return (self.s, cid(self.z + (1 if dim == '+' else -1), self.y, self.c))
    def at(self, flips, z):
        s = 1 - self.s if 'x' in flips else self.s
        y = 1 - self.y if 'y' in flips else self.y
        c = 1 - self.c if 'c' in flips else self.c
        return cid(z, y, c) + (s * self.g.ctx if 'x' in self.order else 0)
    def zpush(self, src, b, z, side):
        ok = self.z < self.g.depth - 1 if side == '+' else self.z > 0
        @pl.when(ok)
        def _():
            self.push(src, b, self.dev(side), self.zsend.at[0 if side == '+' else 1, z])
    def start(self):
        own = self.at('', self.z)
        for side in '+-':
            self.zpush(self.own(), own, self.z, side)
        for dim in self.rest + 'c':
            self.push(self.own(), own, self.dev(dim), self.send)
        pltpu.make_async_copy(self.own(), self.view(own), self.local).start()
    def sides(self, d, body):
        if isinstance(d, int) and d == 0:
            body(self.z, '')
            return
        @pl.when(self.z - d >= 0)
        def _():
            body(self.z - d, '-')
        @pl.when(self.z + d < self.g.depth)
        def _():
            body(self.z + d, '+')
    def line(self, d):
        def go(z, side):
            b = self.at('', z)
            self.wait(b)
            self.zpush(self.view(b), b, z, '+' if side == '-' else '-')
            for k in self.rest + 'c':
                self.push(self.view(b), b, self.dev(k), self.send)
        self.sides(d, go)
    def cross(self, flips, dims, d):
        def go(z, side):
            b = self.at(flips, z)
            self.wait(b)
            for k in dims:
                self.push(self.view(b), b, self.dev(k), self.send)
        self.sides(d, go)
    def step(self, t):
        r = self.rest
        if t < self.g.depth:
            self.line(t)
        if 1 <= t <= self.g.depth:
            self.cross(r[0], r[1:] + 'c', t - 1)
        if len(r) > 1:
            if 1 <= t <= self.g.depth:
                self.cross(r[1], 'c', t - 1)
            if 2 <= t <= self.g.depth + 1:
                self.cross(r, 'c', t - 2)
    def steps(self):
        return self.g.depth + len(self.rest)
    def finish(self):
        r = self.rest
        sets = ['', r[0]] + ([r[1], r] if len(r) > 1 else [])
        for f in sets:
            def go(k, f=f):
                self.wait(self.at(f + 'c', k))
            each(self.g.depth, go)
        self.wait(self.at('', self.z), self.local)
        def sent(k):
            for side in '+-':
                n = 0 if side == '+' else 1
                ok = (jnp.logical_and(self.z < self.g.depth - 1, k <= self.z) if side == '+'
                      else jnp.logical_and(self.z > 0, k >= self.z))
                @pl.when(ok)
                def _():
                    self.wait(self.at('', k), self.zsend.at[n, k])
        each(self.g.depth, sent)
        p = self.g.depth
        n = p + (2 * p if len(r) > 1 else 0) + (4 * p if len(r) > 1 else 2 * p)
        v = self.dst.at[pl.ds(0, n)] if self.cols is None else self.dst.at[pl.ds(0, n), :, self.cols]
        pltpu.make_async_copy(v, v, self.send).wait()

def run_gathers(jobs):
    for job in jobs: job.start()
    for t in range(1, max(j.steps() for j in jobs)):
        for job in jobs:
            job.step(t)
    for job in jobs: job.finish()

def gather_kernel(grid, plan, n_in, *refs):
    ins, outs = refs[:n_in], refs[n_in:2 * n_in]
    send, zsend, recv, local = refs[2 * n_in:]
    greet(grid, any('x' in p[1] for p in plan))
    jobs = [Gather(grid, ins[i], outs[i], send.at[j], zsend.at[j], recv.at[j], local.at[j], order, cols) for j, (i, order, cols) in enumerate(plan)]
    run_gathers(jobs)

def gather_sems(grid, plan):
    n = max(grid.ctx * (grid.seqs if 'x' in order else 1) for _, order, _ in plan)
    k = len(plan)
    return [pltpu.SemaphoreType.DMA((k,)), pltpu.SemaphoreType.DMA((k, 2, grid.depth)), pltpu.SemaphoreType.DMA((k, n)), pltpu.SemaphoreType.DMA((k,))]

def gather(grid, arrays, plan, name, cid_):
    full = {}
    for i, order, cols in plan:
        full[i] = grid.ctx * (grid.seqs if 'x' in order else 1)
    outs = [jax.ShapeDtypeStruct((full[i],) + a.shape[1:], a.dtype) for i, a in enumerate(arrays)]
    return pl.pallas_call(
        functools.partial(gather_kernel, grid, plan, len(arrays)),
        out_shape=outs,
        in_specs=[pl.BlockSpec(memory_space=pltpu.VMEM)] * len(arrays),
        out_specs=[pl.BlockSpec(memory_space=pl.ANY)] * len(arrays),
        scratch_shapes=gather_sems(grid, plan),
        compiler_params=pltpu.CompilerParams(collective_id=cid_, has_side_effects=True),
        name=name,
    )(*arrays)
from jax.sharding import PartitionSpec as P

def f32(x):
    return x.astype(jnp.float32)

class Scatter:
    def __init__(self, grid, src, out, bufs, send, zsend, recvs, order):
        self.g, self.src, self.out = grid, src, out
        self.bufc, self.buf1, self.buf2, self.bufz = bufs
        self.send, self.zsend, self.order = send, zsend, order
        self.rc, self.r1, self.r2, self.rz = recvs
        self.dims = order[:0:-1]
        self.two = len(self.dims) > 1
        self.s, self.z, self.y, self.c = grid.here()
    at = Gather.at
    dev = Gather.dev
    def flips(self, f):
        return ''.join(d for d, on in zip(self.dims, f) if on)
    def idx(self, f, z):
        k = 0
        for on in f:
            k = k * 2 + on
        return k * self.g.depth + z
    def push(self, src, dst, recv, dim):
        pltpu.make_async_remote_copy(src, dst, self.send, recv, device_id=self.dev(dim), device_id_type=MESH).start()
    def wait(self, ref, sem):
        pltpu.make_async_copy(ref, ref, sem).wait()
    def combos(self):
        return [(1, 1), (1, 0), (0, 1), (0, 0)] if self.two else [(1,), (0,)]
    def far(self, d, body):
        @pl.when(self.z + d < self.g.depth)
        def _():
            body(self.z + d, '+')
        @pl.when(self.z >= d)
        def _():
            body(self.z - d, '-')
    def start(self):
        for f in self.combos():
            def go(z, side, f=f):
                k = self.idx(f, z)
                self.push(self.src.at[self.at(self.flips(f) + 'c', z)], self.bufc.at[k], self.rc.at[k], 'c')
            def loop(k, _, go=go):
                self.far(self.g.depth - 1 - k, go)
                return _
            lax.fori_loop(0, self.g.depth - 1, loop, None)
            go(self.z, '')
    def stage1(self, f, d):
        def go(z, side):
            k = self.idx(f, z)
            buf = self.bufc.at[k]
            self.wait(buf, self.rc.at[k])
            buf[...] = (f32(self.src[self.at(self.flips(f), z)]) + f32(buf[...])).astype(buf.dtype)
            j = self.idx(f[1:], z)
            self.push(buf, self.buf1.at[j], self.r1.at[j], self.dims[0])
        self.far(d, go) if d is not None else go(self.z, '')
    def stage2(self, d):
        def go(z, side):
            k, j = self.idx((0, 1), z), self.idx((1,), z)
            bufc, buf = self.bufc.at[k], self.buf1.at[j]
            self.wait(bufc, self.rc.at[k])
            self.wait(buf, self.r1.at[j])
            buf[...] = (f32(self.src[self.at(self.dims[1], z)]) + f32(bufc[...]) + f32(buf[...])).astype(buf.dtype)
            self.push(buf, self.buf2.at[z], self.r2.at[z], self.dims[1])
        self.far(d, go) if d is not None else go(self.z, '')
    def merged(self, z):
        k = self.idx((0,) * len(self.dims), z)
        bufc, buf1 = self.bufc.at[k], self.buf1.at[z]
        self.wait(bufc, self.rc.at[k])
        self.wait(buf1, self.r1.at[z])
        acc = f32(self.src[self.at('', z)]) + f32(bufc[...]) + f32(buf1[...])
        if self.two:
            buf2 = self.buf2.at[z]
            self.wait(buf2, self.r2.at[z])
            acc = acc + f32(buf2[...])
        return acc, bufc
    def chain(self, d):
        top = self.g.depth - 1
        def go(zz, side):
            n = 0 if side == '+' else 1
            more = self.z > 0 if side == '+' else self.z < top
            acc, keep = self.merged(zz)
            keep[...] = acc.astype(keep.dtype)
            buf = self.bufz.at[n, zz]
            @pl.when(more)
            def _():
                self.wait(buf, self.rz.at[n, zz])
                keep[...] = (f32(keep[...]) + f32(buf[...])).astype(keep.dtype)
            pltpu.make_async_remote_copy(keep, buf, self.zsend.at[n, zz], self.rz.at[n, zz], device_id=self.dev(side), device_id_type=MESH).start()
        self.far(d, go)
    def total(self):
        top = self.g.depth - 1
        acc, _ = self.merged(self.z)
        self.out[0] = acc
        for n, ok in ((0, self.z > 0), (1, self.z < top)):
            @pl.when(ok)
            def _(n=n):
                buf = self.bufz.at[n, self.z]
                self.wait(buf, self.rz.at[n, self.z])
                self.out[0] += f32(buf[...])
    def finish(self):
        def sent(k):
            for n, ok in ((0, k > self.z), (1, k < self.z)):
                @pl.when(ok)
                def _(n=n):
                    self.wait(self.bufz.at[n, k], self.zsend.at[n, k])
        each(self.g.depth, sent)
        p = self.g.depth
        n = (4 + 2 + 1) * p if self.two else (2 + 1) * p
        v = self.src.at[pl.ds(0, n)]
        self.wait(v, self.send)

def run_scatters(jobs):
    depth = jobs[0].g.depth
    for job in jobs: job.start()
    def sweep(step, own):
        def loop(k, _):
            for job in jobs: step(job, depth - 1 - k)
            return _
        lax.fori_loop(0, depth - 1, loop, None)
        for job in jobs: own(job)
    sweep(lambda j, d: j.stage1(j.combos()[0], d), lambda j: j.stage1(j.combos()[0], None))
    sweep(lambda j, d: j.stage1((1, 0), d) if j.two else None, lambda j: j.stage1((1, 0), None) if j.two else None)
    sweep(lambda j, d: j.stage2(d) if j.two else None, lambda j: j.stage2(None) if j.two else None)
    sweep(lambda j, d: j.chain(d), lambda j: j.total())
    for job in jobs: job.finish()

def scatter_scratch(grid, shape, dtype, order):
    p = grid.depth
    two = len(order) > 2
    n1, nc = (2 * p, 4 * p) if two else (p, 2 * p)
    D = pltpu.SemaphoreType.DMA
    return [pltpu.VMEM((nc,) + shape, dtype), pltpu.VMEM((n1,) + shape, dtype), pltpu.VMEM((p if two else 1,) + (shape if two else (8, 128)), dtype), pltpu.VMEM((2, p) + shape, dtype),
            D(()), D((2, p)), D((nc,)), D((n1,)), D((p,)), D((2, p))]

def scatter_kernel(grid, orders, *refs):
    m = len(orders)
    ins, outs, rest = refs[:m], refs[m:2 * m], refs[2 * m:]
    greet(grid, any('x' in o for o in orders))
    jobs = []
    for j, order in enumerate(orders):
        r = rest[10 * j:10 * j + 10]
        jobs.append(Scatter(grid, ins[j], outs[j], r[:4], r[4], r[5], r[6:10], order))
    run_scatters(jobs)

def scatter(grid, arrays, orders, name, cid_):
    scratch = []
    for a, o in zip(arrays, orders):
        scratch += scatter_scratch(grid, a.shape[1:], a.dtype, o)
    V = pl.BlockSpec(memory_space=pltpu.VMEM)
    return pl.pallas_call(
        functools.partial(scatter_kernel, grid, tuple(orders)),
        out_shape=[jax.ShapeDtypeStruct((1,) + a.shape[1:], jnp.float32) for a in arrays],
        in_specs=[V] * len(arrays), out_specs=[V] * len(arrays),
        scratch_shapes=scratch,
        compiler_params=pltpu.CompilerParams(collective_id=cid_, has_side_effects=True, vmem_limit_bytes=60 * 2**20),
        name=name,
    )(*arrays)

def pair_stack(x, half):
    lane = lax.broadcasted_iota(jnp.int32, x.shape, 1)
    zero = jnp.zeros_like(x)
    return jnp.concatenate((jnp.where(lane < half, x, zero), jnp.where(lane < half, zero, x)), axis=0)

def pair_join(x, half):
    r = x.shape[0] // 2
    lane = lax.broadcasted_iota(jnp.int32, (r, x.shape[1]), 1)
    return jnp.where(lane < half, x[:r], x[r:])

def nt(a, b):
    return lax.dot_general(a, b, (((1,), (1,)), ((), ())), preferred_element_type=jnp.float32)

def nn(a, b):
    return lax.dot_general(a, b, (((1,), (0,)), ((), ())), preferred_element_type=jnp.float32)

def tn(a, b):
    return lax.dot_general(a, b, (((0,), (0,)), ((), ())), preferred_element_type=jnp.float32)

def as_row(col):
    return jnp.transpose(jnp.broadcast_to(col, (col.shape[0], 128)))[0:1]

MASKED = -1e30

def forward_kernel(half, tiles, len_ref, q_ref, k_ref, v_ref, o_ref, lse_ref, top_ref, sum_ref, acc_ref):
    t = pl.program_id(1)
    q2 = pair_stack(q_ref[...], half)
    s = nt(q2, k_ref[...])
    wide = s.shape[1]
    col = lax.broadcasted_iota(jnp.int32, (1, wide), 1) + t * wide
    s = jnp.where(col < len_ref[0], s, MASKED)
    top = jnp.max(s, axis=1, keepdims=True)
    if tiles > 1:
        old = jnp.where(t == 0, MASKED, top_ref[...])
        top = jnp.maximum(old, top)
    p = jnp.exp(s - top)
    total = jnp.sum(p, axis=1, keepdims=True)
    acc = nn(p.astype(jnp.bfloat16), v_ref[...])
    if tiles > 1:
        factor = jnp.where(t == 0, 0.0, jnp.exp(old - top))
        total = total + jnp.where(t == 0, 0.0, sum_ref[...]) * factor
        acc = acc + jnp.where(t == 0, 0.0, acc_ref[...]) * factor
        top_ref[...], sum_ref[...], acc_ref[...] = top, total, acc
    @pl.when(t == tiles - 1)
    def _():
        o_ref[...] = pair_join(acc / total, half)
        lse_ref[0] = as_row(top + jnp.log(total))

def attend(q, k, v, length, heads, tile):
    rows, width = q.shape
    size = width // heads
    total, pairs = k.shape[0], heads // 2
    tiles = total // tile
    wide = 2 * size
    return pl.pallas_call(
        functools.partial(forward_kernel, size, tiles),
        grid_spec=pltpu.PrefetchScalarGridSpec(
            num_scalar_prefetch=1, grid=(pairs, tiles),
            in_specs=[pl.BlockSpec((rows, wide), lambda p, t, n: (0, p)),
                      pl.BlockSpec((tile, wide), lambda p, t, n: (t, p)),
                      pl.BlockSpec((tile, wide), lambda p, t, n: (t, p))],
            out_specs=[pl.BlockSpec((rows, wide), lambda p, t, n: (0, p)),
                       pl.BlockSpec((1, 1, 2 * rows), lambda p, t, n: (p, 0, 0))],
            scratch_shapes=[pltpu.VMEM((2 * rows, 1), jnp.float32), pltpu.VMEM((2 * rows, 1), jnp.float32), pltpu.VMEM((2 * rows, wide), jnp.float32)]),
        out_shape=[jax.ShapeDtypeStruct((rows, width), jnp.float32), jax.ShapeDtypeStruct((pairs, 1, 2 * rows), jnp.float32)],
        name="attend",
    )(length, q, k, v)

def backward_kernel(half, tiles, scale, len_ref, q_ref, k_ref, v_ref, g_ref, o_ref, lse_ref, dq_ref, dk_ref, dv_ref, acc_ref):
    t = pl.program_id(1)
    q2 = pair_stack(q_ref[...], half)
    g2 = pair_stack(g_ref[...], half)
    k, v = k_ref[...], v_ref[...]
    prod = pair_stack(g_ref[...].astype(jnp.float32) * o_ref[...], half)
    delta = jnp.sum(jnp.transpose(prod), axis=0, keepdims=True)
    s = nt(k, q2)
    row = lax.broadcasted_iota(jnp.int32, (s.shape[0], 1), 0) + t * s.shape[0]
    p = jnp.where(row < len_ref[0], jnp.exp(s - lse_ref[0]), 0.0)
    dp = nt(v, g2)
    ds = (p * (dp - delta)).astype(jnp.bfloat16)
    dk_ref[...] = nn(ds, q2).astype(jnp.bfloat16)
    dv_ref[...] = nn(p.astype(jnp.bfloat16), g2).astype(jnp.bfloat16)
    dq = tn(ds, k)
    if tiles > 1:
        dq = dq + jnp.where(t == 0, 0.0, acc_ref[...])
        acc_ref[...] = dq
    @pl.when(t == tiles - 1)
    def _():
        dq_ref[...] = (pair_join(dq, half) * scale).astype(jnp.bfloat16)

def attend_back(q, k, v, g, o, lse, length, heads, tile):
    rows, width = q.shape
    size = width // heads
    total, pairs = k.shape[0], heads // 2
    tiles = total // tile
    wide = 2 * size
    R = pl.BlockSpec((rows, wide), lambda p, t, n: (0, p))
    K = pl.BlockSpec((tile, wide), lambda p, t, n: (t, p))
    return pl.pallas_call(
        functools.partial(backward_kernel, size, tiles, size ** -0.5),
        grid_spec=pltpu.PrefetchScalarGridSpec(
            num_scalar_prefetch=1, grid=(pairs, tiles),
            in_specs=[R, K, K, R, R, pl.BlockSpec((1, 1, 2 * rows), lambda p, t, n: (p, 0, 0))],
            out_specs=[R, K, K],
            scratch_shapes=[pltpu.VMEM((2 * rows, wide), jnp.float32)]),
        out_shape=[jax.ShapeDtypeStruct((rows, width), jnp.bfloat16)] + [jax.ShapeDtypeStruct((total, width), jnp.bfloat16)] * 2,
        name="attend_back",
    )(length, q, k, v, g, o, lse)
HEADS = 12
EPSILON = 1e-12
ROOM = 52 * 2**20

def normalize(u):
    mean = jnp.mean(u, axis=-1, keepdims=True)
    centred = u - mean
    r = lax.rsqrt(jnp.mean(centred * centred, axis=-1, keepdims=True) + EPSILON)
    return centred * r, r

def normalize_back(e, n, r, gain):
    c = e * gain
    return r * (c - jnp.mean(c, axis=-1, keepdims=True) - n * jnp.mean(c * n, axis=-1, keepdims=True))

def gelu_parts(v):
    cdf = 0.5 * (1.0 + lax.erf(v * (0.5 ** 0.5)))
    slope = cdf + v * jnp.exp(-0.5 * v * v) * ((2 * jnp.pi) ** -0.5)
    return v * cdf, slope

def padded(shape, dtype):
    sub = 32 // jnp.dtype(dtype).itemsize // 1 if False else (8 if jnp.dtype(dtype).itemsize == 4 else 16)
    return math.prod(shape[:-2]) * (-(-shape[-2] // sub) * sub) * (-(-shape[-1] // 128) * 128) * jnp.dtype(dtype).itemsize

def reduce_blocks(grid, arrays, orders, name, cid_):
    need = sum(padded(a.shape, a.dtype) * 3 for a in arrays)
    if need <= ROOM + 20 * 2**20 and grid.depth <= 4:
        return scatter(grid, arrays, orders, name, cid_)
    out = []
    for a, order in zip(arrays, orders):
        axes = ("seq", "ctx") if "x" in order else "ctx"
        out.append(lax.psum_scatter(a.astype(jnp.float32), axes, scatter_dimension=0, tiled=True))
    return out

def per_device(grid, inputs, lengths, cotangent, w_qkv, w_out, w_in, w_back, vectors, ffn_bias):
    bf, f4 = jnp.bfloat16, jnp.float32
    rows_in = inputs[0]
    rows, width = rows_in.shape
    hidden_size = w_in.shape[1]
    devices = grid.seqs * grid.ctx
    part, part_ff = w_qkv.shape[0], w_back.shape[0]
    slots = grid.ctx * rows
    scale = (width // HEADS) ** -0.5

    small = jnp.concatenate((jnp.pad(vectors.T, ((0, 0), (0, 128 - part))), jnp.pad(ffn_bias[None], ((0, 7), (0, 128 - part_ff)))), axis=0)[None]
    half = 3 * width // 2
    qkv_all, small_all = gather(grid, [w_qkv[None], small], [(0, "zyx", pl.ds(0, half)), (0, "zxy", pl.ds(half, half)), (1, "zyx", None)], "gather_qkv", 0)
    qkv_full = qkv_all.reshape(width, 3 * width)
    vec = small_all[:, :8, :part].transpose(1, 0, 2).reshape(8, width).astype(f4)
    ffn_full = small_all[:, 8, :part_ff].reshape(1, hidden_size).astype(f4)

    projected = jnp.dot(rows_in, qkv_full, preferred_element_type=f4)
    query = (projected[:, :width] + vec[0]).astype(bf)
    key = projected[:, width:2 * width].astype(bf)
    value = (projected[:, 2 * width:] + vec[1]).astype(bf)
    key_all, value_all, out_all, in_all, back_all = gather(
        grid, [key[None], value[None], w_out[None], w_in[None], w_back[None]],
        [(0, "zy", None), (1, "zy", None), (2, "zyx", None), (3, "zyx", None), (4, "zxy", None)], "gather_rest", 1)
    key_all, value_all = key_all.reshape(slots, width), value_all.reshape(slots, width)
    out_full, in_full, back_full = out_all.reshape(width, width), in_all.reshape(width, hidden_size), back_all.reshape(hidden_size, width)

    tile = min(slots, 2048)
    query_scaled = query * jnp.asarray(scale, bf)
    attended_f, lse = attend(query_scaled, key_all, value_all, lengths, HEADS, tile)
    attended = attended_f.astype(bf)
    branch = jnp.dot(attended, out_full, preferred_element_type=f4) + vec[2]
    norm_one, r_one = normalize(rows_in.astype(f4) + branch)
    first = norm_one * vec[3] + vec[4]
    first_low = first.astype(bf)
    hidden = jnp.dot(first_low, in_full, preferred_element_type=f4) + ffn_full
    active_f, slope = gelu_parts(hidden)
    active = active_f.astype(bf)
    second = jnp.dot(active, back_full, preferred_element_type=f4) + vec[5]
    norm_two, r_two = normalize(first + second)
    result = (norm_two * vec[6] + vec[7]).astype(bf)
    start = lax.axis_index("ctx") * rows
    valid = (start + jnp.arange(rows, dtype=jnp.int32) < lengths[0]).astype(f4)[:, None]
    grad_result = cotangent[0].astype(f4) * valid
    grad_second = normalize_back(grad_result, norm_two, r_two, vec[6])
    grad_second_low = grad_second.astype(bf)
    grad_active = lax.dot_general(grad_second_low, back_full, (((1,), (1,)), ((), ())), preferred_element_type=f4)
    grad_hidden = (grad_active * slope).astype(bf)
    grad_first = grad_second + lax.dot_general(grad_hidden, in_full, (((1,), (1,)), ((), ())), preferred_element_type=f4)
    grad_branch_full = normalize_back(grad_first, norm_one, r_one, vec[3])
    grad_branch = grad_branch_full.astype(bf)
    grad_attended = lax.dot_general(grad_branch, out_full, (((1,), (1,)), ((), ())), preferred_element_type=f4).astype(bf)

    def outer(a, b):
        return lax.dot_general(a, b, (((0,), (0,)), ((), ())), preferred_element_type=f4).astype(bf)
    g_back = outer(active, grad_second_low).reshape(devices, part_ff, width)
    g_in = outer(first_low, grad_hidden).reshape(devices, part, hidden_size)
    g_out = outer(attended, grad_branch).reshape(devices, part, width)
    grad_query, g_key, g_value = attend_back(query_scaled, key_all, value_all, grad_attended, attended_f, lse, lengths, HEADS, tile)
    own_key, own_value, d_out, d_in, d_back = reduce_blocks(
        grid, [g_key.reshape(grid.ctx, rows, width), g_value.reshape(grid.ctx, rows, width), g_out, g_in, g_back],
        ["zy", "zy", "zyx", "zyx", "zxy"], "reduce_rest", 2)
    grad_projected = jnp.concatenate((grad_query, own_key[0].astype(bf), own_value[0].astype(bf)), axis=1)
    g_qkv = outer(rows_in, grad_projected).reshape(devices, part, 3 * width)
    grad_inputs = grad_branch_full + lax.dot_general(grad_projected, qkv_full, (((1,), (1,)), ((), ())), preferred_element_type=f4)
    sums = jnp.stack((
        jnp.sum(grad_query.astype(f4), axis=0), jnp.sum(own_value[0].astype(bf).astype(f4), axis=0),
        jnp.sum(grad_branch.astype(f4), axis=0), jnp.sum(grad_first * norm_one, axis=0), jnp.sum(grad_first, axis=0),
        jnp.sum(grad_second_low.astype(f4), axis=0), jnp.sum(grad_result * norm_two, axis=0), jnp.sum(grad_result, axis=0)))
    grad_ffn = jnp.sum(grad_hidden.astype(f4), axis=0)
    blocks = jnp.pad(sums.reshape(8, devices, part).transpose(1, 0, 2), ((0, 0), (0, 0), (0, 128 - part)))
    ffn_blocks = jnp.pad(grad_ffn.reshape(devices, 1, part_ff), ((0, 0), (0, 7), (0, 128 - part_ff)))
    g_small = jnp.concatenate((blocks, ffn_blocks), axis=1)
    d_qkv_a, d_qkv_b, d_small = reduce_blocks(grid, [g_qkv[:, :, :half], g_qkv[:, :, half:], g_small], ["zyx", "zxy", "zyx"], "reduce_qkv", 3)
    d_qkv = jnp.concatenate((d_qkv_a[0], d_qkv_b[0]), axis=1)
    return (result[None], grad_inputs[None], d_qkv, d_out[0], d_in[0], d_back[0], d_small[0, :8, :part].T, d_small[0, 8, :part_ff])

def solution(mesh):
    grid = Grid(mesh.shape["seq"], mesh.shape["ctx"])
    split, both = P("seq", "ctx", None), P(("seq", "ctx"), None)
    return jax.shard_map(
        functools.partial(per_device, grid), mesh=mesh,
        in_specs=(split, P("seq"), split, both, both, both, both, both, P(("seq", "ctx"))),
        out_specs=(split, split, both, both, both, both, both, P(("seq", "ctx"))),
        check_vma=False,
    )
```

time: 1050 us -> 333 us (0.32)
  waiting for transfers between devices: 776 us -> 0 us
  Pallas kernels: 0 us -> 278 us
  blocking collectives: 123 us -> 0 us
  matrix products: 81.4 us -> 29.7 us
  local copies, waits for them, and re-layouts: 35 us -> 9.09 us
  between operations: 14.8 us -> 1.76 us
    reduce_scatter x4 -> x0, waiting for transfers between devices: 428 us -> none  [the longest x1 142 us: per_device(): lax.psum_scatter(grad_w_in, ('seq', 'ctx'), scatter_dimension=0, tiled=True)]
    pallas_call x0 -> x6, Pallas kernels: none -> 278 us  [the longest x2 147 us: scatter(): pl.pallas_call(functools.partial(scatter_kernel, grid, tuple(orders)), ou...]
    all_gather x6 -> x0, waiting for transfers between devices: 221 us -> none  [the longest x1 63.2 us: per_device(): lax.all_gather(w_in, ('seq', 'ctx'), axis=0, tiled=True)]
    unnamed x12 -> x0, waiting for transfers between devices: 127 us -> none
    unnamed x2 -> x0, blocking collectives: 79.7 us -> none
    dot_general x18 -> x12, matrix products: 81.4 us -> 29.7 us  [the longest x4 9.86 us: outer(): lax.dot_general(a, b, (((0,), (0,)), ((), ())), preferred_element_type=f4)]
    all_gather x1 -> x0, blocking collectives: 43.8 us -> none  [per_device(): lax.all_gather(vectors, ('seq', 'ctx'), axis=0, tiled=True)]
    unnamed x47 -> x55, local copies, waits for them, and re-layouts: 16.7 us -> 2.57 us
  transfers between devices with their start and end apart: 11 -> 0, of which waited for: 11 -> 0; matrix products, arithmetic and copies ran while one was open for 8% -> 0% of each run, Pallas kernels for 0% -> 0%
where the time goes in v1:
time: 333 us; the launch traced here: 332 us
  Pallas kernels  278 us (83%)
  matrix products  29.7 us (9%)
  other arithmetic  13.8 us (4%)
  local copies, waits for them, and re-layouts  9.09 us (3%)
    pallas_call x2, Pallas kernels, scatter(): pl.pallas_call(functools.partial(scatter_kernel, grid, tuple(orders)), ou...  147 us
    pallas_call x2, Pallas kernels, gather(): pl.pallas_call(functools.partial(gather_kernel, grid, plan, len(arrays)),...  110 us
    pallas_call x1, Pallas kernels, attend_back(): pl.pallas_call(functools.partial(backward_kernel, size, tiles, size ** (-...  11.7 us
    dot_general x4, matrix products, outer(): lax.dot_general(a, b, (((0,), (0,)), ((), ())), preferred_element_type=f4)  9.86 us
    pallas_call x1, Pallas kernels, attend(): pl.pallas_call(functools.partial(forward_kernel, size, tiles), grid_spec=...  9.25 us

profile of v1, /device:TPU:0, one launch (start us, length us, event | category | flops | bytes accessed | tf_op | source)
XLA Modules:
  0.0 332.2 jit_solution(4034752027464614637)
XLA Ops:
  0.6 1.3 fusion.32.refs_1_
  1.9 27.8 %gather_qkv.1 = (bf16[32,24,2304]{2,1,0:T(8,128)(2,1)}, bf16[32,16,128]{2,1,0:T(8,128)(2,1)}) custom-call(bf16[1,24,2304]{2,1,0:T(8,128)(2,1)} %bitcast.112, bf16[1,16,128]{2,1,0:T(8,128)(2,1)} %fusion.32.refs_1_), custom_call_target="tpu_custom_call" | custom-call | tf_op jit(solution)/shard_map/gather_qkv/pallas_call | solution.py:168
  29.7 0.9 convert_bitcast_fusion.2
  31.0 2.8 convolution_bitcast_fusion
  33.9 0.8 fusion.22
  35.4 82.3 %gather_rest.1 = (bf16[16,128,768]{2,1,0:T(8,128)(2,1)}, bf16[16,128,768]{2,1,0:T(8,128)(2,1)}, bf16[32,24,768]{2,1,0:T(8,128)(2,1)}, bf16[32,24,3072]{2,1,0:T(8,128)(2,1)}, bf16[32,96,768]{2,1,0:T(8,128)(2,1)}) custom-call(bf16[1,128,768]{2,1,0:T(8,128)(2,1)} %get-tuple-element.73.refs_0_, bf16[1,128,768]{2,1,0:T(8,128)(2,1)} %fusion.24.refs_1_, ...), custom_call_target="tpu_custom_call" | custom-call | tf_op jit(solution)/shard_map/gather_rest/pallas_call | solution.py:168
  117.7 0.9 convert_reduce_fusion.5
  119.4 9.3 %attend.1 = (f32[128,768]{1,0:T(8,128)}, f32[6,1,256]{2,1,0:T(1,128)}) custom-call(s32[1]{0:T(128)} %copy.31.len_ref, bf16[128,768]{1,0:T(8,128)(2,1)} %get-tuple-element.72.q_ref, bf16[2048,768]{1,0:T(8,128)(2,1)} %bitcast.94, bf16[2048,768]{1,0:T(8,128)(2,1)} %bitcast.96), custom_call_target="tpu_custom_call" | custom-call | tf_op jit(solution)/shard_map/attend/pallas_call | solution.py:389
  128.7 1.4 fusion.43
  130.5 3.3 %convolution_add_fusion = f32[128,3072]{1,0:T(8,128)S(1)} fusion(bf16[768,3072]{1,0:T(8,128)(2,1)} %bitcast.87, f32[3072]{0:T(1024)S(1)} %reshape.162, f32[128,768]{1,0:T(8,128)S(1)} %get-tuple-element.76, f32[768]{0:T(1024)S(1)} %add.134, f32[768]{0:T(1024)S(1)} %mul.152, f32[128]{0:T(128)S(1)} %add_rsqrt_fusion.1, f32[128]{0:T(128)S(1)} %broadcast_multiply_fusion.5), kind=kOutput, calls=%fused_computation.5 | convolution fusion | flops 604864512 | bytes 6704128 | tf_op jit(solution)/shard_map/dot_general | solution.py:511
  134.3 1.0 fusion.44
  135.7 0.8 fusion.19
  136.6 1.5 convert_reduce_fusion.1
  138.1 4.7 %convert_reduce_fusion = (f32[3072]{0:T(1024)}, bf16[128,3072]{1,0:T(8,128)(2,1)S(1)}) fusion(f32[128,3072]{1,0:T(8,128)S(1)} %convolution_add_fusion, bf16[3072,768]{1,0:T(8,128)(2,1)} %bitcast.99, f32[128,768]{1,0:T(8,128)S(1)} %get-tuple-element.65), kind=kOutput, calls=%fused_computation.12 | convolution fusion | flops 608793600 | bytes 7483392 | tf_op jit(solution)/shard_map/dot_general | solution.py:522
  142.8 2.3 multiply_reduce_fusion
  145.2 1.5 convert_reduce_fusion.2
  146.7 1.2 convolution_convert_fusion.4.g_ref
  147.9 11.7 %attend_back.1 = (bf16[128,768]{1,0:T(8,128)(2,1)}, bf16[2048,768]{1,0:T(8,128)(2,1)}, bf16[2048,768]{1,0:T(8,128)(2,1)}) custom-call(s32[1]{0:T(128)} %copy.31.len_ref, bf16[128,768]{1,0:T(8,128)(2,1)} %get-tuple-element.72.q_ref, bf16[2048,768]{1,0:T(8,128)(2,1)} %bitcast.95, bf16[2048,768]{1,0:T(8,128)(2,1)} %bitcast.97, ...), custom_call_target="tpu_custom_call" | custom-call | tf_op jit(solution)/shard_map/attend_back/pallas_call | solution.py:433
  159.7 1.5 convolution_convert_fusion.3
  161.2 3.6 %convolution_convert_fusion.2 = bf16[768,3072]{1,0:T(8,128)(2,1)} fusion(bf16[128,3072]{1,0:T(8,128)(2,1)S(1)} %copy-done.6, f32[128,768]{1,0:T(8,128)S(1)} %get-tuple-element.76, f32[768]{0:T(1024)S(1)} %add.134, f32[768]{0:T(1024)S(1)} %mul.152, f32[128]{0:T(128)S(1)} %copy-done.15, f32[128]{0:T(128)S(1)} %broadcast_multiply_fusion.5), kind=kOutput, calls=%fused_computation.2 | convolution fusion | flops 606830592 | bytes 5905408 | tf_op jit(solution)/shard_map/dot_general | solution.py:530
  164.8 3.6 %convolution_convert_fusion.1 = bf16[3072,768]{1,0:T(8,128)(2,1)} fusion(f32[128,768]{1,0:T(8,128)S(1)} %get-tuple-element.65, f32[128,3072]{1,0:T(8,128)S(1)} %convolution_add_fusion), kind=kOutput, calls=%fused_computation.1 | convolution fusion | flops 608403456 | bytes 6684672 | tf_op jit(solution)/shard_map/dot_general | solution.py:530
  168.4 114.1 %reduce_rest.1 = (f32[1,128,768]{2,1,0:T(8,128)}, f32[1,128,768]{2,1,0:T(8,128)}, f32[1,24,768]{2,1,0:T(8,128)}, f32[1,24,3072]{2,1,0:T(8,128)}, f32[1,96,768]{2,1,0:T(8,128)}) custom-call(bf16[16,128,768]{2,1,0:T(8,128)(2,1)} %bitcast.103, bf16[16,128,768]{2,1,0:T(8,128)(2,1)} %bitcast.104, bf16[32,24,768]{2,1,0:T(8,128)(2,1)} %bitcast.98, ...), custom_call_target="tpu_custom_call" | custom-call | tf_op jit(solution)/shard_map/reduce_rest/pallas_call | solution.py:326
  282.5 1.6 convert_reduce_fusion.3
  284.2 1.0 convert_bitcast_fusion.1
  285.2 3.0 fusion.6
  288.2 1.1 convolution_convert_fusion
  289.5 2.0 fusion.42
  292.6 0.7 select_maximum_fusion.refs_2_
  293.3 32.7 %reduce_qkv.1 = (f32[1,24,1152]{2,1,0:T(8,128)}, f32[1,24,1152]{2,1,0:T(8,128)}, f32[1,16,128]{2,1,0:T(8,128)}) custom-call(bf16[32,24,1152]{2,1,0:T(8,128)(2,1)} %get-tuple-element.71.refs_0_, bf16[32,24,1152]{2,1,0:T(8,128)(2,1)} %get-tuple-element.70.refs_1_, f32[32,16,128]{2,1,0:T(8,128)} %select_maximum_fusion.refs_2_), custom_call_target="tpu_custom_call" | custom-call | tf_op jit(solution)/shard_map/reduce_qkv/pallas_call | solution.py:326
  326.1 1.7 pad_maximum_fusion.3
  327.7 1.3 slice_bitcast_fusion
  329.0 1.2 slice_bitcast_fusion.1
  (88 shorter events, 5.7 us)
Async XLA Ops:
  119.4 9.3 %copy-start.2 = (bf16[32,24,768]{2,1,0:T(8,128)(2,1)S(1)}, bf16[32,24,768]{2,1,0:T(8,128)(2,1)}, u32[]{:S(2)}) copy-start(bf16[32,24,768]{2,1,0:T(8,128)(2,1)} %get-tuple-element.33) | copy-start | bytes 3538948
  119.4 9.3 %copy-start.7 = (bf16[1,128,768]{2,1,0:T(8,128)(2,1)S(1)}, bf16[1,128,768]{2,1,0:T(8,128)(2,1)}, u32[]{:S(2)}) copy-start(bf16[1,128,768]{2,1,0:T(8,128)(2,1)} %param.9) | copy-start | bytes 589828
  130.5 12.3 %copy-start.14 = (f32[128]{0:T(128)}, f32[128]{0:T(128)S(1)}, u32[]{:S(2)}) copy-start(f32[128]{0:T(128)S(1)} %add_rsqrt_fusion.1) | copy-start | bytes 1540
  130.5 3.8 %copy-start.1 = (bf16[32,96,768]{2,1,0:T(8,128)(2,1)S(1)}, bf16[32,96,768]{2,1,0:T(8,128)(2,1)}, u32[]{:S(2)}) copy-start(bf16[32,96,768]{2,1,0:T(8,128)(2,1)} %get-tuple-element.35) | copy-start | bytes 14155780
  134.3 1.4 copy-start.10
  136.6 6.2 %slice-start = ((s8[4718592]{0:T(1024)(128)(4,1)}), s8[4194304]{0:T(1024)(128)(4,1)S(1)}, s32[]{:S(2)}) async-start(s8[4718592]{0:T(1024)(128)(4,1)} %bitcast.88), calls=%async_computation | async-start | bytes 8388608
  138.1 4.7 %slice-start.1 = ((s8[4718592]{0:T(1024)(128)(4,1)}), s8[524288]{0:T(1024)(128)(4,1)S(1)}, s32[]{:S(2)}) async-start(s8[4718592]{0:T(1024)(128)(4,1)} %bitcast.88), calls=%async_computation.1 | async-start | bytes 1048576
  142.8 2.4 copy-start.5
  145.2 1.5 copy-start.3
  147.9 11.7 %copy-start.4 = (f32[128,768]{1,0:T(8,128)S(1)}, f32[128,768]{1,0:T(8,128)}, u32[]{:S(2)}) copy-start(f32[128,768]{1,0:T(8,128)} %get-tuple-element.32.o_ref) | copy-start | bytes 1179652
  159.7 1.5 copy-start.6
  159.7 1.5 copy-start.15
  168.4 116.8 %copy-start = (bf16[32,24,2304]{2,1,0:T(8,128)(2,1)S(1)}, bf16[32,24,2304]{2,1,0:T(8,128)(2,1)}, u32[]{:S(2)}) copy-start(bf16[32,24,2304]{2,1,0:T(8,128)(2,1)} %get-tuple-element.28) | copy-start | bytes 10616836
  285.2 3.0 copy-start.8
  289.4 2.1 copy-start.23
  289.4 2.2 copy-start.9
  289.4 2.3 copy-start.20
  289.4 2.4 copy-start.19
  289.4 2.5 copy-start.22
  289.4 2.6 copy-start.21
  289.4 2.7 copy-start.18
  289.4 2.8 copy-start.17
  289.4 2.9 copy-start.16
  293.3 36.9 %copy-start.13 = (f32[1,24,768]{2,1,0:T(8,128)S(1)}, f32[1,24,768]{2,1,0:T(8,128)}, u32[]{:S(2)}) copy-start(f32[1,24,768]{2,1,0:T(8,128)} %get-tuple-element.44) | copy-start | bytes 221188
  293.3 37.5 %copy-start.12 = (f32[1,24,3072]{2,1,0:T(8,128)S(1)}, f32[1,24,3072]{2,1,0:T(8,128)}, u32[]{:S(2)}) copy-start(f32[1,24,3072]{2,1,0:T(8,128)} %get-tuple-element.45) | copy-start | bytes 884740
  293.3 38.2 %copy-start.11 = (f32[1,96,768]{2,1,0:T(8,128)S(1)}, f32[1,96,768]{2,1,0:T(8,128)}, u32[]{:S(2)}) copy-start(f32[1,96,768]{2,1,0:T(8,128)} %get-tuple-element.46) | copy-start | bytes 884740

commit v2 on v1

--- a/solution.py
+++ b/solution.py
@@ -294,10 +294,12 @@
             return _
         lax.fori_loop(0, depth - 1, loop, None)
         for job in jobs: own(job)
+    def late(j, d):
+        j.stage2(d) if j.two else j.chain(d)
     sweep(lambda j, d: j.stage1(j.combos()[0], d), lambda j: j.stage1(j.combos()[0], None))
     sweep(lambda j, d: j.stage1((1, 0), d) if j.two else None, lambda j: j.stage1((1, 0), None) if j.two else None)
-    sweep(lambda j, d: j.stage2(d) if j.two else None, lambda j: j.stage2(None) if j.two else None)
-    sweep(lambda j, d: j.chain(d), lambda j: j.total())
+    sweep(late, lambda j: j.stage2(None) if j.two else j.total())
+    sweep(lambda j, d: j.chain(d) if j.two else None, lambda j: j.total() if j.two else None)
     for job in jobs: job.finish()
 
 def scatter_scratch(grid, shape, dtype, order):
@@ -496,7 +498,7 @@
     value = (projected[:, 2 * width:] + vec[1]).astype(bf)
     key_all, value_all, out_all, in_all, back_all = gather(
         grid, [key[None], value[None], w_out[None], w_in[None], w_back[None]],
-        [(0, "zy", None), (1, "zy", None), (2, "zyx", None), (3, "zyx", None), (4, "zxy", None)], "gather_rest", 1)
+        [(0, "zy", None), (1, "zy", None), (2, "zyx", None), (3, "zyx", None), (4, "zyx", None)], "gather_rest", 1)
     key_all, value_all = key_all.reshape(slots, width), value_all.reshape(slots, width)
     out_full, in_full, back_full = out_all.reshape(width, width), in_all.reshape(width, hidden_size), back_all.reshape(hidden_size, width)
 
@@ -534,7 +536,7 @@
     grad_query, g_key, g_value = attend_back(query_scaled, key_all, value_all, grad_attended, attended_f, lse, lengths, HEADS, tile)
     own_key, own_value, d_out, d_in, d_back = reduce_blocks(
         grid, [g_key.reshape(grid.ctx, rows, width), g_value.reshape(grid.ctx, rows, width), g_out, g_in, g_back],
-        ["zy", "zy", "zyx", "zyx", "zxy"], "reduce_rest", 2)
+        ["zy", "zy", "zyx", "zyx", "zyx"], "reduce_rest", 2)
     grad_projected = jnp.concatenate((grad_query, own_key[0].astype(bf), own_value[0].astype(bf)), axis=1)
     g_qkv = outer(rows_in, grad_projected).reshape(devices, part, 3 * width)
     grad_inputs = grad_branch_full + lax.dot_general(grad_projected, qkv_full, (((1,), (1,)), ((), ())), preferred_element_type=f4)

time: 333 us -> 287 us (0.86)
  Pallas kernels: 278 us -> 231 us
    pallas_call x2, Pallas kernels: 147 us -> 108 us  [scatter(): pl.pallas_call(functools.partial(scatter_kernel, grid, tuple(orders)), ou...]
    pallas_call x2, Pallas kernels: 110 us -> 103 us  [gather(): pl.pallas_call(functools.partial(gather_kernel, grid, plan, len(arrays)),...]
where the time goes in v2:
time: 287 us; the launch traced here: 286 us
  Pallas kernels  231 us (80%)
  matrix products  29.7 us (10%)
  other arithmetic  13.8 us (5%)
  local copies, waits for them, and re-layouts  9.09 us (3%)
    pallas_call x2, Pallas kernels, scatter(): pl.pallas_call(functools.partial(scatter_kernel, grid, tuple(orders)), ou...  108 us
    pallas_call x2, Pallas kernels, gather(): pl.pallas_call(functools.partial(gather_kernel, grid, plan, len(arrays)),...  103 us
    pallas_call x1, Pallas kernels, attend_back(): pl.pallas_call(functools.partial(backward_kernel, size, tiles, size ** (-...  11.7 us
    dot_general x4, matrix products, outer(): lax.dot_general(a, b, (((0,), (0,)), ((), ())), preferred_element_type=f4)  9.86 us
    pallas_call x1, Pallas kernels, attend(): pl.pallas_call(functools.partial(forward_kernel, size, tiles), grid_spec=...  9.25 us

profile of v2, /device:TPU:0, one launch (start us, length us, event | category | flops | bytes accessed | tf_op | source)
XLA Modules:
  0.0 285.8 jit_solution(16233588765436342110)
XLA Ops:
  0.6 1.3 fusion.32.refs_1_
  1.9 27.8 %gather_qkv.1 = (bf16[32,24,2304]{2,1,0:T(8,128)(2,1)}, bf16[32,16,128]{2,1,0:T(8,128)(2,1)}) custom-call(bf16[1,24,2304]{2,1,0:T(8,128)(2,1)} %bitcast.112, bf16[1,16,128]{2,1,0:T(8,128)(2,1)} %fusion.32.refs_1_), custom_call_target="tpu_custom_call" | custom-call | tf_op jit(solution)/shard_map/gather_qkv/pallas_call | solution.py:168
  29.7 0.9 convert_bitcast_fusion.2
  31.0 2.8 convolution_bitcast_fusion
  33.9 0.8 fusion.22
  35.4 75.1 %gather_rest.1 = (bf16[16,128,768]{2,1,0:T(8,128)(2,1)}, bf16[16,128,768]{2,1,0:T(8,128)(2,1)}, bf16[32,24,768]{2,1,0:T(8,128)(2,1)}, bf16[32,24,3072]{2,1,0:T(8,128)(2,1)}, bf16[32,96,768]{2,1,0:T(8,128)(2,1)}) custom-call(bf16[1,128,768]{2,1,0:T(8,128)(2,1)} %get-tuple-element.73.refs_0_, bf16[1,128,768]{2,1,0:T(8,128)(2,1)} %fusion.24.refs_1_, ...), custom_call_target="tpu_custom_call" | custom-call | tf_op jit(solution)/shard_map/gather_rest/pallas_call | solution.py:168
  110.5 0.9 convert_reduce_fusion.5
  112.3 9.3 %attend.1 = (f32[128,768]{1,0:T(8,128)}, f32[6,1,256]{2,1,0:T(1,128)}) custom-call(s32[1]{0:T(128)} %copy.31.len_ref, bf16[128,768]{1,0:T(8,128)(2,1)} %get-tuple-element.72.q_ref, bf16[2048,768]{1,0:T(8,128)(2,1)} %bitcast.94, bf16[2048,768]{1,0:T(8,128)(2,1)} %bitcast.96), custom_call_target="tpu_custom_call" | custom-call | tf_op jit(solution)/shard_map/attend/pallas_call | solution.py:391
  121.5 1.4 fusion.43
  123.4 3.3 %convolution_add_fusion = f32[128,3072]{1,0:T(8,128)S(1)} fusion(bf16[768,3072]{1,0:T(8,128)(2,1)} %bitcast.87, f32[3072]{0:T(1024)S(1)} %reshape.162, f32[128,768]{1,0:T(8,128)S(1)} %get-tuple-element.76, f32[768]{0:T(1024)S(1)} %add.134, f32[768]{0:T(1024)S(1)} %mul.152, f32[128]{0:T(128)S(1)} %add_rsqrt_fusion.1, f32[128]{0:T(128)S(1)} %broadcast_multiply_fusion.5), kind=kOutput, calls=%fused_computation.5 | convolution fusion | flops 604864512 | bytes 6704128 | tf_op jit(solution)/shard_map/dot_general | solution.py:513
  127.1 1.0 fusion.44
  128.5 0.8 fusion.19
  129.4 1.5 convert_reduce_fusion.1
  130.9 4.7 %convert_reduce_fusion = (f32[3072]{0:T(1024)}, bf16[128,3072]{1,0:T(8,128)(2,1)S(1)}) fusion(f32[128,3072]{1,0:T(8,128)S(1)} %convolution_add_fusion, bf16[3072,768]{1,0:T(8,128)(2,1)} %bitcast.99, f32[128,768]{1,0:T(8,128)S(1)} %get-tuple-element.65), kind=kOutput, calls=%fused_computation.12 | convolution fusion | flops 608793600 | bytes 7483392 | tf_op jit(solution)/shard_map/dot_general | solution.py:524
  135.7 2.3 multiply_reduce_fusion
  138.0 1.5 convert_reduce_fusion.2
  139.5 1.2 convolution_convert_fusion.4.g_ref
  140.8 11.7 %attend_back.1 = (bf16[128,768]{1,0:T(8,128)(2,1)}, bf16[2048,768]{1,0:T(8,128)(2,1)}, bf16[2048,768]{1,0:T(8,128)(2,1)}) custom-call(s32[1]{0:T(128)} %copy.31.len_ref, bf16[128,768]{1,0:T(8,128)(2,1)} %get-tuple-element.72.q_ref, bf16[2048,768]{1,0:T(8,128)(2,1)} %bitcast.95, bf16[2048,768]{1,0:T(8,128)(2,1)} %bitcast.97, ...), custom_call_target="tpu_custom_call" | custom-call | tf_op jit(solution)/shard_map/attend_back/pallas_call | solution.py:435
  152.5 1.5 convolution_convert_fusion.3
  154.0 3.6 %convolution_convert_fusion.2 = bf16[768,3072]{1,0:T(8,128)(2,1)} fusion(bf16[128,3072]{1,0:T(8,128)(2,1)S(1)} %copy-done.6, f32[128,768]{1,0:T(8,128)S(1)} %get-tuple-element.76, f32[768]{0:T(1024)S(1)} %add.134, f32[768]{0:T(1024)S(1)} %mul.152, f32[128]{0:T(128)S(1)} %copy-done.15, f32[128]{0:T(128)S(1)} %broadcast_multiply_fusion.5), kind=kOutput, calls=%fused_computation.2 | convolution fusion | flops 606830592 | bytes 5905408 | tf_op jit(solution)/shard_map/dot_general | solution.py:532
  157.6 3.6 %convolution_convert_fusion.1 = bf16[3072,768]{1,0:T(8,128)(2,1)} fusion(f32[128,768]{1,0:T(8,128)S(1)} %get-tuple-element.65, f32[128,3072]{1,0:T(8,128)S(1)} %convolution_add_fusion), kind=kOutput, calls=%fused_computation.1 | convolution fusion | flops 608403456 | bytes 6684672 | tf_op jit(solution)/shard_map/dot_general | solution.py:532
  161.3 75.8 %reduce_rest.1 = (f32[1,128,768]{2,1,0:T(8,128)}, f32[1,128,768]{2,1,0:T(8,128)}, f32[1,24,768]{2,1,0:T(8,128)}, f32[1,24,3072]{2,1,0:T(8,128)}, f32[1,96,768]{2,1,0:T(8,128)}) custom-call(bf16[16,128,768]{2,1,0:T(8,128)(2,1)} %bitcast.103, bf16[16,128,768]{2,1,0:T(8,128)(2,1)} %bitcast.104, bf16[32,24,768]{2,1,0:T(8,128)(2,1)} %bitcast.98, ...), custom_call_target="tpu_custom_call" | custom-call | tf_op jit(solution)/shard_map/reduce_rest/pallas_call | solution.py:328
  237.1 1.6 convert_reduce_fusion.3
  238.7 1.0 convert_bitcast_fusion.1
  239.8 3.0 %fusion.6 = f32[1,128,768]{2,1,0:T(8,128)} fusion(f32[128,768]{1,0:T(8,128)S(1)} %get-tuple-element.67, bf16[768,2304]{1,0:T(8,128)(2,1)S(1)} %bitcast.92, bf16[128,768]{1,0:T(8,128)(2,1)S(1)} %get-tuple-element.69, bf16[128,768]{1,0:T(8,128)(2,1)S(1)} %convert_bitcast_fusion.1, bf16[128,768]{1,0:T(8,128)(2,1)} %get-tuple-element.37), kind=kOutput, calls=%fused_computation.19 | convolution fusion | flops 454852608 | bytes 4915200 | tf_op jit(solution)/shard_map/dot_general | solution.py:542
  242.8 1.1 convolution_convert_fusion
  244.0 2.0 fusion.42
  247.1 0.7 select_maximum_fusion.refs_2_
  247.9 31.7 %reduce_qkv.1 = (f32[1,24,1152]{2,1,0:T(8,128)}, f32[1,24,1152]{2,1,0:T(8,128)}, f32[1,16,128]{2,1,0:T(8,128)}) custom-call(bf16[32,24,1152]{2,1,0:T(8,128)(2,1)} %get-tuple-element.71.refs_0_, bf16[32,24,1152]{2,1,0:T(8,128)(2,1)} %get-tuple-element.70.refs_1_, f32[32,16,128]{2,1,0:T(8,128)} %select_maximum_fusion.refs_2_), custom_call_target="tpu_custom_call" | custom-call | tf_op jit(solution)/shard_map/reduce_qkv/pallas_call | solution.py:328
  279.6 1.7 pad_maximum_fusion.3
  281.3 1.3 slice_bitcast_fusion
  282.5 1.2 slice_bitcast_fusion.1
  (88 shorter events, 5.7 us)
Async XLA Ops:
  112.2 9.3 %copy-start.2 = (bf16[32,24,768]{2,1,0:T(8,128)(2,1)S(1)}, bf16[32,24,768]{2,1,0:T(8,128)(2,1)}, u32[]{:S(2)}) copy-start(bf16[32,24,768]{2,1,0:T(8,128)(2,1)} %get-tuple-element.33) | copy-start | bytes 3538948
  112.3 9.3 %copy-start.7 = (bf16[1,128,768]{2,1,0:T(8,128)(2,1)S(1)}, bf16[1,128,768]{2,1,0:T(8,128)(2,1)}, u32[]{:S(2)}) copy-start(bf16[1,128,768]{2,1,0:T(8,128)(2,1)} %param.9) | copy-start | bytes 589828
  123.3 12.3 %copy-start.14 = (f32[128]{0:T(128)}, f32[128]{0:T(128)S(1)}, u32[]{:S(2)}) copy-start(f32[128]{0:T(128)S(1)} %add_rsqrt_fusion.1) | copy-start | bytes 1540
  123.4 3.8 %copy-start.1 = (bf16[32,96,768]{2,1,0:T(8,128)(2,1)S(1)}, bf16[32,96,768]{2,1,0:T(8,128)(2,1)}, u32[]{:S(2)}) copy-start(bf16[32,96,768]{2,1,0:T(8,128)(2,1)} %get-tuple-element.35) | copy-start | bytes 14155780
  127.1 1.4 copy-start.10
  129.4 6.2 %slice-start = ((s8[4718592]{0:T(1024)(128)(4,1)}), s8[4194304]{0:T(1024)(128)(4,1)S(1)}, s32[]{:S(2)}) async-start(s8[4718592]{0:T(1024)(128)(4,1)} %bitcast.88), calls=%async_computation | async-start | bytes 8388608
  130.9 4.7 %slice-start.1 = ((s8[4718592]{0:T(1024)(128)(4,1)}), s8[524288]{0:T(1024)(128)(4,1)S(1)}, s32[]{:S(2)}) async-start(s8[4718592]{0:T(1024)(128)(4,1)} %bitcast.88), calls=%async_computation.1 | async-start | bytes 1048576
  135.6 2.4 copy-start.5
  138.0 1.5 copy-start.3
  140.8 11.7 %copy-start.4 = (f32[128,768]{1,0:T(8,128)S(1)}, f32[128,768]{1,0:T(8,128)}, u32[]{:S(2)}) copy-start(f32[128,768]{1,0:T(8,128)} %get-tuple-element.32.o_ref) | copy-start | bytes 1179652
  152.5 1.5 copy-start.6
  152.5 1.5 copy-start.15
  161.3 78.5 %copy-start = (bf16[32,24,2304]{2,1,0:T(8,128)(2,1)S(1)}, bf16[32,24,2304]{2,1,0:T(8,128)(2,1)}, u32[]{:S(2)}) copy-start(bf16[32,24,2304]{2,1,0:T(8,128)(2,1)} %get-tuple-element.28) | copy-start | bytes 10616836
  239.7 3.0 %copy-start.8 = (bf16[128,768]{1,0:T(8,128)(2,1)S(1)}, bf16[128,768]{1,0:T(8,128)(2,1)}, u32[]{:S(2)}) copy-start(bf16[128,768]{1,0:T(8,128)(2,1)} %get-tuple-element.37) | copy-start | bytes 589828
  243.9 2.1 copy-start.23
  243.9 2.2 copy-start.9
  243.9 2.3 copy-start.20
  243.9 2.4 copy-start.19
  243.9 2.5 copy-start.22
  243.9 2.6 copy-start.21
  244.0 2.7 copy-start.18
  244.0 2.8 copy-start.17
  244.0 2.9 copy-start.16
  247.9 35.9 %copy-start.13 = (f32[1,24,768]{2,1,0:T(8,128)S(1)}, f32[1,24,768]{2,1,0:T(8,128)}, u32[]{:S(2)}) copy-start(f32[1,24,768]{2,1,0:T(8,128)} %get-tuple-element.44) | copy-start | bytes 221188
  247.9 36.5 %copy-start.12 = (f32[1,24,3072]{2,1,0:T(8,128)S(1)}, f32[1,24,3072]{2,1,0:T(8,128)}, u32[]{:S(2)}) copy-start(f32[1,24,3072]{2,1,0:T(8,128)} %get-tuple-element.45) | copy-start | bytes 884740
  247.9 37.2 %copy-start.11 = (f32[1,96,768]{2,1,0:T(8,128)S(1)}, f32[1,96,768]{2,1,0:T(8,128)}, u32[]{:S(2)}) copy-start(f32[1,96,768]{2,1,0:T(8,128)} %get-tuple-element.46) | copy-start | bytes 884740

commit v3 on v1

--- a/solution.py
+++ b/solution.py
@@ -44,16 +44,23 @@
         lax.fori_loop(0, n, lambda k, _: (body(k), None)[1], None)
 
 class Gather:
-    def __init__(self, grid, src, dst, send, zsend, recv, local, order, cols=None):
+    def __init__(self, grid, src, dst, sems, order, cols=None):
         self.g, self.src, self.dst = grid, src, dst
-        self.send, self.zsend, self.recv, self.local, self.order = send, zsend, recv, local, order
-        self.cols = cols
+        self.send, self.zsend, self.recv, self.local = sems
+        self.order, self.cols = order, cols
         self.s, self.z, self.y, self.c = grid.here()
         self.rest = order[1:]
+    def rows(self, start, n):
+        if len(self.dst.shape) == 3:
+            return self.dst.at[start] if n is None else self.dst.at[pl.ds(start, n)]
+        size = self.src.shape[-2]
+        span = pl.ds(pl.multiple_of(start * size, 8), size * (n or 1))
+        return self.dst.at[span] if self.cols is None else self.dst.at[span, self.cols]
     def view(self, b):
-        return self.dst.at[b] if self.cols is None else self.dst.at[b, :, self.cols]
+        return self.rows(b, None)
     def own(self):
-        return self.src.at[0] if self.cols is None else self.src.at[0, :, self.cols]
+        src = self.src.at[0] if len(self.src.shape) == 3 else self.src
+        return src if self.cols is None else src.at[:, self.cols]
     def push(self, src, b, dev, sem):
         pltpu.make_async_remote_copy(src, self.view(b), sem, self.recv.at[b], device_id=dev, device_id_type=MESH).start()
     def wait(self, b, sem=None):
@@ -74,11 +81,11 @@
         @pl.when(ok)
         def _():
             self.push(src, b, self.dev(side), self.zsend.at[0 if side == '+' else 1, z])
-    def start(self):
+    def start(self, dims=None):
         own = self.at('', self.z)
         for side in '+-':
             self.zpush(self.own(), own, self.z, side)
-        for dim in self.rest + 'c':
+        for dim in dims or self.rest + 'c':
             self.push(self.own(), own, self.dev(dim), self.send)
         pltpu.make_async_copy(self.own(), self.view(own), self.local).start()
     def sides(self, d, body):
@@ -91,13 +98,18 @@
         @pl.when(self.z + d < self.g.depth)
         def _():
             body(self.z + d, '+')
-    def line(self, d):
+    def line(self, d, dims=None):
         def go(z, side):
             b = self.at('', z)
             self.wait(b)
             self.zpush(self.view(b), b, z, '+' if side == '-' else '-')
-            for k in self.rest + 'c':
+            for k in dims or self.rest + 'c':
                 self.push(self.view(b), b, self.dev(k), self.send)
+        self.sides(d, go)
+    def late(self, dim, d):
+        def go(z, side):
+            b = self.at('', z)
+            self.push(self.own() if side == '' else self.view(b), b, self.dev(dim), self.send)
         self.sides(d, go)
     def cross(self, flips, dims, d):
         def go(z, side):
@@ -119,7 +131,7 @@
                 self.cross(r, 'c', t - 2)
     def steps(self):
         return self.g.depth + len(self.rest)
-    def finish(self):
+    def arrive(self):
         r = self.rest
         sets = ['', r[0]] + ([r[1], r] if len(r) > 1 else [])
         for f in sets:
@@ -127,6 +139,7 @@
                 self.wait(self.at(f + 'c', k))
             each(self.g.depth, go)
         self.wait(self.at('', self.z), self.local)
+    def leave(self):
         def sent(k):
             for side in '+-':
                 n = 0 if side == '+' else 1
@@ -137,51 +150,77 @@
                     self.wait(self.at('', k), self.zsend.at[n, k])
         each(self.g.depth, sent)
         p = self.g.depth
-        n = p + (2 * p if len(r) > 1 else 0) + (4 * p if len(r) > 1 else 2 * p)
-        v = self.dst.at[pl.ds(0, n)] if self.cols is None else self.dst.at[pl.ds(0, n), :, self.cols]
+        n = p + (2 * p + 4 * p if len(self.rest) > 1 else 2 * p)
+        v = self.rows(0, n)
         pltpu.make_async_copy(v, v, self.send).wait()
 
-def run_gathers(jobs):
-    for job in jobs: job.start()
-    for t in range(1, max(j.steps() for j in jobs)):
-        for job in jobs:
-            job.step(t)
-    for job in jobs: job.finish()
-
-def gather_kernel(grid, plan, n_in, *refs):
-    ins, outs = refs[:n_in], refs[n_in:2 * n_in]
-    send, zsend, recv, local = refs[2 * n_in:]
-    greet(grid, any('x' in p[1] for p in plan))
-    jobs = [Gather(grid, ins[i], outs[i], send.at[j], zsend.at[j], recv.at[j], local.at[j], order, cols) for j, (i, order, cols) in enumerate(plan)]
-    run_gathers(jobs)
-
-def gather_sems(grid, plan):
-    n = max(grid.ctx * (grid.seqs if 'x' in order else 1) for _, order, _ in plan)
-    k = len(plan)
-    return [pltpu.SemaphoreType.DMA((k,)), pltpu.SemaphoreType.DMA((k, 2, grid.depth)), pltpu.SemaphoreType.DMA((k, n)), pltpu.SemaphoreType.DMA((k,))]
-
-def gather(grid, arrays, plan, name, cid_):
-    full = {}
-    for i, order, cols in plan:
-        full[i] = grid.ctx * (grid.seqs if 'x' in order else 1)
-    outs = [jax.ShapeDtypeStruct((full[i],) + a.shape[1:], a.dtype) for i, a in enumerate(arrays)]
+PLAN = ("q0", "q1", "q2", "q3", "w0", "q4", "w1", "q5", "qa", "k0", "k1", "w2", "k2", "w3", "k3", "w4", "k4", "w5")
+
+def fetch_kernel(grid, scale, *refs):
+    x, w_qkv, vec, w_bias, w_out, w_in, w_back = refs[:7]
+    qkv_all, vec_all, bias_all, out_all, in_all, back_all, key_all, value_all, query = refs[7:16]
+    key, value = refs[16:18]
+    sems = refs[18:]
+    greet(grid, True)
+    def job(i, src, dst, order, cols=None):
+        return Gather(grid, src, dst, [r.at[i] for r in sems], order, cols)
+    width = x.shape[1]
+    half = 3 * width // 2
+    parts = {
+        "q": [job(0, vec, vec_all, "zyx"), job(1, w_qkv, qkv_all, "zyx", pl.ds(0, half)), job(2, w_qkv, qkv_all, "zxy", pl.ds(half, half))],
+        "w": [job(3, w_bias, bias_all, "zyx"), job(4, w_out, out_all, "zyx"), job(5, w_in, in_all, "zyx"), job(6, w_back, back_all, "zyx")],
+        "k": [job(7, key, key_all, "zy"), job(8, value, value_all, "zy")]}
+    for word in PLAN:
+        jobs, t = parts[word[0]], word[1]
+        for j in jobs:
+            if t == "a": j.arrive()
+            elif t == "s": j.start("xc")
+            elif t == "l": j.line(int(word[2]), "xc")
+            elif t == "y": j.late("y", int(word[2]))
+            elif t == "b": j.cross("y", "xc", int(word[2]))
+            elif t == "x": j.cross("x", "c", int(word[2]))
+            elif t == "z": j.cross("yx", "c", int(word[2]))
+            elif t == "0": j.start()
+            else: j.step(int(t))
+        if word == "qa":
+            lane = lax.broadcasted_iota(jnp.int32, (16, 128), 1)
+            pick = (lane == lax.broadcasted_iota(jnp.int32, (16, 128), 0)).astype(jnp.bfloat16)
+            rows = nt(pick, vec_all[...])
+            key[...] = nn(x[...], qkv_all[:, width:2 * width]).astype(jnp.bfloat16)
+            value[...] = (nn(x[...], qkv_all[:, 2 * width:]) + rows[1:2]).astype(jnp.bfloat16)
+    q = (nn(x[...], qkv_all[:, :width]) + rows[0:1]).astype(jnp.bfloat16)
+    query[...] = q * jnp.asarray(scale, jnp.bfloat16)
+    for j in parts["k"] + parts["w"]:
+        j.arrive()
+    for j in parts["q"] + parts["k"] + parts["w"]:
+        j.leave()
+
+def fetch(grid, x, w_qkv, vec, w_bias, w_out, w_in, w_back, scale):
+    devices, bf = grid.seqs * grid.ctx, jnp.bfloat16
+    rows, width = x.shape
+    S = jax.ShapeDtypeStruct
+    V, A = pl.BlockSpec(memory_space=pltpu.VMEM), pl.BlockSpec(memory_space=pl.ANY)
+    D = pltpu.SemaphoreType.DMA
+    flat = lambda a: S((devices * a.shape[-2], a.shape[-1]), bf)
+    deep = lambda a: S((devices,) + a.shape[1:], bf)
+    kv = S((grid.ctx * rows, width), bf)
     return pl.pallas_call(
-        functools.partial(gather_kernel, grid, plan, len(arrays)),
-        out_shape=outs,
-        in_specs=[pl.BlockSpec(memory_space=pltpu.VMEM)] * len(arrays),
-        out_specs=[pl.BlockSpec(memory_space=pl.ANY)] * len(arrays),
-        scratch_shapes=gather_sems(grid, plan),
-        compiler_params=pltpu.CompilerParams(collective_id=cid_, has_side_effects=True),
-        name=name,
-    )(*arrays)
+        functools.partial(fetch_kernel, grid, scale),
+        out_shape=[flat(w_qkv), flat(vec), deep(w_bias), deep(w_out), deep(w_in), deep(w_back), kv, kv, S((rows, width), bf)],
+        in_specs=[V] * 7,
+        out_specs=[V, V] + [A] * 6 + [V],
+        scratch_shapes=[pltpu.VMEM((rows, width), bf)] * 2 + [D((9,)), D((9, 2, grid.depth)), D((9, devices)), D((9,))],
+        compiler_params=pltpu.CompilerParams(collective_id=0, has_side_effects=True, vmem_limit_bytes=60 * 2**20),
+        name="fetch",
+    )(x, w_qkv, vec, w_bias, w_out, w_in, w_back)
 from jax.sharding import PartitionSpec as P
 
 def f32(x):
     return x.astype(jnp.float32)
 
 class Scatter:
-    def __init__(self, grid, src, out, bufs, send, zsend, recvs, order):
-        self.g, self.src, self.out = grid, src, out
+    def __init__(self, grid, src, out, bufs, send, zsend, recvs, order, mine=None, local=None):
+        self.g, self.src, self.out, self.mine, self.local = grid, src, out, mine, local
         self.bufc, self.buf1, self.buf2, self.bufz = bufs
         self.send, self.zsend, self.order = send, zsend, order
         self.rc, self.r1, self.r2, self.rz = recvs
@@ -210,6 +249,15 @@
         @pl.when(self.z >= d)
         def _():
             body(self.z - d, '-')
+    def own(self, f, z):
+        return self.src[self.at(self.flips(f), z)] if self.mine is None else self.mine[self.idx(f, z)]
+    def load(self):
+        for f in self.combos():
+            def go(z, f=f):
+                pltpu.make_async_copy(self.src.at[self.at(self.flips(f), z)], self.mine.at[self.idx(f, z)], self.local).start()
+            each(self.g.depth, go)
+    def loaded(self):
+        pltpu.make_async_copy(self.mine, self.mine, self.local).wait()
     def start(self):
         for f in self.combos():
             def go(z, side, f=f):
@@ -225,7 +273,7 @@
             k = self.idx(f, z)
             buf = self.bufc.at[k]
             self.wait(buf, self.rc.at[k])
-            buf[...] = (f32(self.src[self.at(self.flips(f), z)]) + f32(buf[...])).astype(buf.dtype)
+            buf[...] = (f32(self.own(f, z)) + f32(buf[...])).astype(buf.dtype)
             j = self.idx(f[1:], z)
             self.push(buf, self.buf1.at[j], self.r1.at[j], self.dims[0])
         self.far(d, go) if d is not None else go(self.z, '')
@@ -235,7 +283,7 @@
             bufc, buf = self.bufc.at[k], self.buf1.at[j]
             self.wait(bufc, self.rc.at[k])
             self.wait(buf, self.r1.at[j])
-            buf[...] = (f32(self.src[self.at(self.dims[1], z)]) + f32(bufc[...]) + f32(buf[...])).astype(buf.dtype)
+            buf[...] = (f32(self.own((0, 1), z)) + f32(bufc[...]) + f32(buf[...])).astype(buf.dtype)
             self.push(buf, self.buf2.at[z], self.r2.at[z], self.dims[1])
         self.far(d, go) if d is not None else go(self.z, '')
     def merged(self, z):
@@ -243,7 +291,7 @@
         bufc, buf1 = self.bufc.at[k], self.buf1.at[z]
         self.wait(bufc, self.rc.at[k])
         self.wait(buf1, self.r1.at[z])
-        acc = f32(self.src[self.at('', z)]) + f32(bufc[...]) + f32(buf1[...])
+        acc = f32(self.own((0,) * len(self.dims), z)) + f32(bufc[...]) + f32(buf1[...])
         if self.two:
             buf2 = self.buf2.at[z]
             self.wait(buf2, self.r2.at[z])
@@ -285,21 +333,6 @@
         v = self.src.at[pl.ds(0, n)]
         self.wait(v, self.send)
 
-def run_scatters(jobs):
-    depth = jobs[0].g.depth
-    for job in jobs: job.start()
-    def sweep(step, own):
-        def loop(k, _):
-            for job in jobs: step(job, depth - 1 - k)
-            return _
-        lax.fori_loop(0, depth - 1, loop, None)
-        for job in jobs: own(job)
-    sweep(lambda j, d: j.stage1(j.combos()[0], d), lambda j: j.stage1(j.combos()[0], None))
-    sweep(lambda j, d: j.stage1((1, 0), d) if j.two else None, lambda j: j.stage1((1, 0), None) if j.two else None)
-    sweep(lambda j, d: j.stage2(d) if j.two else None, lambda j: j.stage2(None) if j.two else None)
-    sweep(lambda j, d: j.chain(d), lambda j: j.total())
-    for job in jobs: job.finish()
-
 def scatter_scratch(grid, shape, dtype, order):
     p = grid.depth
     two = len(order) > 2
@@ -307,30 +340,6 @@
     D = pltpu.SemaphoreType.DMA
     return [pltpu.VMEM((nc,) + shape, dtype), pltpu.VMEM((n1,) + shape, dtype), pltpu.VMEM((p if two else 1,) + (shape if two else (8, 128)), dtype), pltpu.VMEM((2, p) + shape, dtype),
             D(()), D((2, p)), D((nc,)), D((n1,)), D((p,)), D((2, p))]
-
-def scatter_kernel(grid, orders, *refs):
-    m = len(orders)
-    ins, outs, rest = refs[:m], refs[m:2 * m], refs[2 * m:]
-    greet(grid, any('x' in o for o in orders))
-    jobs = []
-    for j, order in enumerate(orders):
-        r = rest[10 * j:10 * j + 10]
-        jobs.append(Scatter(grid, ins[j], outs[j], r[:4], r[4], r[5], r[6:10], order))
-    run_scatters(jobs)
-
-def scatter(grid, arrays, orders, name, cid_):
-    scratch = []
-    for a, o in zip(arrays, orders):
-        scratch += scatter_scratch(grid, a.shape[1:], a.dtype, o)
-    V = pl.BlockSpec(memory_space=pltpu.VMEM)
-    return pl.pallas_call(
-        functools.partial(scatter_kernel, grid, tuple(orders)),
-        out_shape=[jax.ShapeDtypeStruct((1,) + a.shape[1:], jnp.float32) for a in arrays],
-        in_specs=[V] * len(arrays), out_specs=[V] * len(arrays),
-        scratch_shapes=scratch,
-        compiler_params=pltpu.CompilerParams(collective_id=cid_, has_side_effects=True, vmem_limit_bytes=60 * 2**20),
-        name=name,
-    )(*arrays)
 
 def pair_stack(x, half):
     lane = lax.broadcasted_iota(jnp.int32, x.shape, 1)
@@ -400,21 +409,22 @@
         name="attend",
     )(length, q, k, v)
 
-def backward_kernel(half, tiles, scale, len_ref, q_ref, k_ref, v_ref, g_ref, o_ref, lse_ref, dq_ref, dk_ref, dv_ref, acc_ref):
+def backward_math(half, length, start, q, k, v, g, o, lse):
+    q2, g2 = pair_stack(q, half), pair_stack(g, half)
+    delta = jnp.sum(jnp.transpose(pair_stack(f32(g) * o, half)), axis=0, keepdims=True)
+    s = nt(k, q2)
+    row = lax.broadcasted_iota(jnp.int32, (s.shape[0], 1), 0) + start
+    p = jnp.where(row < length, jnp.exp(s - lse), 0.0)
+    ds = (p * (nt(v, g2) - delta)).astype(jnp.bfloat16)
+    return tn(ds, k), nn(ds, q2), nn(p.astype(jnp.bfloat16), g2)
+
+def backward_kernel(half, tiles, scale, len_ref, q_ref, k_ref, v_ref, g_ref, o_ref, lse_ref, dq_ref, dk_ref, dv_ref, sum_ref, acc_ref):
     t = pl.program_id(1)
-    q2 = pair_stack(q_ref[...], half)
-    g2 = pair_stack(g_ref[...], half)
-    k, v = k_ref[...], v_ref[...]
-    prod = pair_stack(g_ref[...].astype(jnp.float32) * o_ref[...], half)
-    delta = jnp.sum(jnp.transpose(prod), axis=0, keepdims=True)
-    s = nt(k, q2)
-    row = lax.broadcasted_iota(jnp.int32, (s.shape[0], 1), 0) + t * s.shape[0]
-    p = jnp.where(row < len_ref[0], jnp.exp(s - lse_ref[0]), 0.0)
-    dp = nt(v, g2)
-    ds = (p * (dp - delta)).astype(jnp.bfloat16)
-    dk_ref[...] = nn(ds, q2).astype(jnp.bfloat16)
-    dv_ref[...] = nn(p.astype(jnp.bfloat16), g2).astype(jnp.bfloat16)
-    dq = tn(ds, k)
+    dq, dk, dv = backward_math(half, len_ref[0], t * k_ref.shape[0], q_ref[...], k_ref[...], v_ref[...], g_ref[...], o_ref[...], lse_ref[0])
+    dk_ref[...] = dk.astype(jnp.bfloat16)
+    dv_ref[...] = dv.astype(jnp.bfloat16)
+    sums = jnp.sum(dv, axis=0, keepdims=True)
+    sum_ref[0] = sums + jnp.where(t == 0, 0.0, sum_ref[0]) if tiles > 1 else sums
     if tiles > 1:
         dq = dq + jnp.where(t == 0, 0.0, acc_ref[...])
         acc_ref[...] = dq
@@ -435,14 +445,134 @@
         grid_spec=pltpu.PrefetchScalarGridSpec(
             num_scalar_prefetch=1, grid=(pairs, tiles),
             in_specs=[R, K, K, R, R, pl.BlockSpec((1, 1, 2 * rows), lambda p, t, n: (p, 0, 0))],
-            out_specs=[R, K, K],
+            out_specs=[R, K, K, pl.BlockSpec((1, 1, wide), lambda p, t, n: (p, 0, 0))],
             scratch_shapes=[pltpu.VMEM((2 * rows, wide), jnp.float32)]),
-        out_shape=[jax.ShapeDtypeStruct((rows, width), jnp.bfloat16)] + [jax.ShapeDtypeStruct((total, width), jnp.bfloat16)] * 2,
+        out_shape=[jax.ShapeDtypeStruct((rows, width), jnp.bfloat16)] + [jax.ShapeDtypeStruct((total, width), jnp.bfloat16)] * 2 + [jax.ShapeDtypeStruct((pairs, 1, wide), jnp.float32)],
         name="attend_back",
     )(length, q, k, v, g, o, lse)
+ORDER = ("ds", "pA", "ld", "d1,*", "As", "A1,*", "pB", "Bs", "B1,*", "d2,*", "e", "A4,*", "B4,d3,*", "g", "qs", "q1,*", "q2,*", "d4,*", "i", "q3,*", "q4,*")
+
+def settle_kernel(grid, size, *refs):
+    length, key_all, value_all, g_out, g_in, g_back, w_qkv, q, g, o, lse, x, base, g_bias, g_vec = refs[:15]
+    d_qkv, d_out, d_in, d_back, d_bias, d_vec, grad_inputs = refs[15:22]
+    own_key, own_value, w_query, w_key, w_value, grads, k_slots, v_slots, wide_w, vec_cols, vec_src, kA, vA, kB, vB = refs[22:37]
+    kv_sem, w_sem, local = refs[37:40]
+    mine = refs[40:43]
+    bufs = refs[43:]
+    rows, width = x.shape
+    third, pair, pairs = width // 2, 2 * size, width // (2 * size)
+    def pull(p):
+        at = pl.multiple_of(p * pair, pair)
+        return [pltpu.make_async_copy(src.at[:, pl.ds(at, pair)], slots.at[lax.rem(p, 2)], kv_sem.at[n, lax.rem(p, 2)])
+                for n, (src, slots) in enumerate(((key_all, k_slots), (value_all, v_slots)))]
+    for copy in pull(0): copy.start()
+    greet(grid, True)
+    cut = lambda n: d_qkv.at[:, :, pl.ds(n * width, width)]
+    part_of = lambda ref, n: ref.at[:, :, pl.ds(n * third, third)]
+    specs = [("A", vA, part_of(own_value, 0), "zy"), ("A", kA, part_of(own_key, 0), "zy"), ("B", vB, part_of(own_value, 1), "zy"), ("B", kB, part_of(own_key, 1), "zy"),
+             ("d", g_back, d_back, "zyx"), ("d", g_in, d_in, "zyx"), ("d", g_out, d_out, "zyx"), ("d", g_bias, d_bias, "zyx"),
+             ("q", vec_src, d_vec, "zyx"), ("q", w_query, cut(0), "zyx"), ("q", w_key, cut(1), "zyx"), ("q", w_value, cut(2), "zxy")]
+    jobs = {"A": [], "B": [], "d": [], "q": []}
+    for n, (group, src, out, order) in enumerate(specs):
+        r = bufs[10 * n:10 * n + 10]
+        extra = (mine[n - 4], local.at[n - 4]) if 4 <= n < 7 else ()
+        jobs[group].append(Scatter(grid, src, out, r[:4], r[4], r[5], r[6:10], order, *extra))
+    big = jobs["d"][:3]
+    def weigh(at, dst):
+        part, wide = dst.shape[1], width // 2
+        for n in range(2):
+            full = tn(x[...], grads[:, at + n * wide:at + (n + 1) * wide])
+            for k in range(dst.shape[0]):
+                dst[k, :, n * wide:(n + 1) * wide] = full[k * part:(k + 1) * part].astype(dst.dtype)
+    lane = lax.broadcasted_iota(jnp.int32, (pair, 128), 1)
+    def attention(first, dk, dv):
+        def one(j, _):
+            p = first + j
+            slot = lax.rem(p, 2)
+            @pl.when(p + 1 < pairs)
+            def _():
+                for copy in pull(p + 1): copy.start()
+            for copy in pull(p): copy.wait()
+            at = pl.ds(pl.multiple_of(p * pair, pair), pair)
+            to = pl.ds(pl.multiple_of(j * pair, pair), pair)
+            dq, dk_part, dv_part = backward_math(size, length[0], 0, q[:, at], k_slots[slot], v_slots[slot], g[:, at], o[:, at], lse[p])
+            dk[:, :, to] = dk_part.astype(dk.dtype).reshape(dk.shape[0], rows, pair)
+            dv[:, :, to] = dv_part.astype(dv.dtype).reshape(dv.shape[0], rows, pair)
+            dq = (pair_join(dq, size) * size ** -0.5).astype(grads.dtype)
+            grads[:, at] = dq
+            tall = lambda v: jnp.transpose(jnp.broadcast_to(jnp.sum(f32(v), axis=0, keepdims=True), (128, pair)))
+            vec_cols[at, :] = jnp.where(lane == 0, tall(dq), jnp.where(lane == 1, tall(dv_part), g_vec[at, :]))
+            return _
+        lax.fori_loop(0, pairs // 2, one, None)
+    def early():
+        weigh(0, w_query)
+        part = vec_src.shape[1]
+        for k in range(vec_src.shape[0]):
+            vec_src[k] = vec_cols[k * part:(k + 1) * part]
+    def after():
+        grads[:, width:2 * width] = own_key[0].astype(grads.dtype)
+        grads[:, 2 * width:] = own_value[0].astype(grads.dtype)
+        weigh(width, w_key)
+        weigh(2 * width, w_value)
+    def inward():
+        total = base[...]
+        for n in range(3):
+            copy = pltpu.make_async_copy(w_qkv.at[:, pl.ds(n * width, width)], wide_w, w_sem)
+            copy.start()
+            copy.wait()
+            total = total + nt(grads[:, n * width:(n + 1) * width], wide_w[...])
+        grad_inputs[...] = total
+    alone = {"pA": lambda: attention(0, kA, vA), "pB": lambda: attention(pairs // 2, kB, vB), "e": early, "g": after, "i": inward,
+             "ld": lambda: [job.loaded() for job in big]}
+    def step(word, d):
+        for job in jobs[word[0]]:
+            if word[1] == "s":
+                if job.mine is not None: job.load()
+                job.start()
+            elif word[1] == "1": job.stage1(job.combos()[0], d)
+            elif word[1] == "2": job.stage1((1, 0), d)
+            elif word[1] == "3": job.stage2(d)
+            elif d is None: job.total()
+            else: job.chain(d)
+    for phase in ORDER:
+        words = phase.split(",")
+        if phase in alone: alone[phase]()
+        elif words[-1] == "*":
+            def loop(k, _, words=words):
+                for word in words[:-1]: step(word, grid.depth - 1 - k)
+                return _
+            lax.fori_loop(0, grid.depth - 1, loop, None)
+            for word in words[:-1]: step(word, None)
+        else:
+            for word in words: step(word, None)
+    for group in [n for n in "ABdq" if n + "s" in ORDER]:
+        for job in jobs[group]: job.finish()
+
+def settle(grid, size, length, key_all, value_all, g_out, g_in, g_back, w_qkv, q, g, o, lse, x, base, g_bias, g_vec):
+    bf, f4 = jnp.bfloat16, jnp.float32
+    rows, width = x.shape
+    part, devices = g_out.shape[1], grid.seqs * grid.ctx
+    slots, pair = key_all.shape[0], 2 * size
+    S = jax.ShapeDtypeStruct
+    V, A = pl.BlockSpec(memory_space=pltpu.VMEM), pl.BlockSpec(memory_space=pl.ANY)
+    D, M = pltpu.SemaphoreType.DMA, pltpu.VMEM
+    scratch = [M((1, rows, width), f4)] * 2 + [M((devices, part, width), bf)] * 3 + [M((rows, 3 * width), bf)] + [M((2, slots, pair), bf)] * 2
+    scratch += [M((width, width), bf), M((width, 128), f4), M((devices, part, 128), f4)] + [M((grid.ctx, rows, width // 2), bf)] * 4
+    scratch += [D((2, 2)), D(()), D((3,))] + [M((devices // 2,) + a.shape[1:], bf) for a in (g_back, g_in, g_out)]
+    for shape, dtype, order in ([((rows, width // 2), bf, "zy")] * 4 + [(a.shape[1:], a.dtype, "zyx") for a in (g_back, g_in, g_out, g_bias)]
+                                + [((part, 128), f4, "zyx"), ((part, width), bf, "zyx"), ((part, width), bf, "zyx"), ((part, width), bf, "zxy")]):
+        scratch += scatter_scratch(grid, shape, dtype, order)
+    one = lambda a: S((1,) + a.shape[1:], f4)
+    return pl.pallas_call(
+        functools.partial(settle_kernel, grid, size),
+        out_shape=[S((1, part, 3 * width), f4), one(g_out), one(g_in), one(g_back), one(g_bias), S((1, part, 128), f4), S((rows, width), f4)],
+        in_specs=[pl.BlockSpec(memory_space=pltpu.SMEM)] + [A] * 6 + [V] * 8, out_specs=[V] * 7, scratch_shapes=scratch,
+        compiler_params=pltpu.CompilerParams(collective_id=1, has_side_effects=True, vmem_limit_bytes=63 * 2**20),
+        name="settle",
+    )(length, key_all, value_all, g_out, g_in, g_back, w_qkv, q, g, o, lse, x, base, g_bias, g_vec)
+
 HEADS = 12
 EPSILON = 1e-12
-ROOM = 52 * 2**20
 
 def normalize(u):
     mean = jnp.mean(u, axis=-1, keepdims=True)
@@ -458,20 +588,6 @@
     cdf = 0.5 * (1.0 + lax.erf(v * (0.5 ** 0.5)))
     slope = cdf + v * jnp.exp(-0.5 * v * v) * ((2 * jnp.pi) ** -0.5)
     return v * cdf, slope
-
-def padded(shape, dtype):
-    sub = 32 // jnp.dtype(dtype).itemsize // 1 if False else (8 if jnp.dtype(dtype).itemsize == 4 else 16)
-    return math.prod(shape[:-2]) * (-(-shape[-2] // sub) * sub) * (-(-shape[-1] // 128) * 128) * jnp.dtype(dtype).itemsize
-
-def reduce_blocks(grid, arrays, orders, name, cid_):
-    need = sum(padded(a.shape, a.dtype) * 3 for a in arrays)
-    if need <= ROOM + 20 * 2**20 and grid.depth <= 4:
-        return scatter(grid, arrays, orders, name, cid_)
-    out = []
-    for a, order in zip(arrays, orders):
-        axes = ("seq", "ctx") if "x" in order else "ctx"
-        out.append(lax.psum_scatter(a.astype(jnp.float32), axes, scatter_dimension=0, tiled=True))
-    return out
 
 def per_device(grid, inputs, lengths, cotangent, w_qkv, w_out, w_in, w_back, vectors, ffn_bias):
     bf, f4 = jnp.bfloat16, jnp.float32
@@ -483,25 +599,28 @@
     slots = grid.ctx * rows
     scale = (width // HEADS) ** -0.5
 
-    small = jnp.concatenate((jnp.pad(vectors.T, ((0, 0), (0, 128 - part))), jnp.pad(ffn_bias[None], ((0, 7), (0, 128 - part_ff)))), axis=0)[None]
     half = 3 * width // 2
-    qkv_all, small_all = gather(grid, [w_qkv[None], small], [(0, "zyx", pl.ds(0, half)), (0, "zxy", pl.ds(half, half)), (1, "zyx", None)], "gather_qkv", 0)
-    qkv_full = qkv_all.reshape(width, 3 * width)
-    vec = small_all[:, :8, :part].transpose(1, 0, 2).reshape(8, width).astype(f4)
-    ffn_full = small_all[:, 8, :part_ff].reshape(1, hidden_size).astype(f4)
-
-    projected = jnp.dot(rows_in, qkv_full, preferred_element_type=f4)
-    query = (projected[:, :width] + vec[0]).astype(bf)
-    key = projected[:, width:2 * width].astype(bf)
-    value = (projected[:, 2 * width:] + vec[1]).astype(bf)
-    key_all, value_all, out_all, in_all, back_all = gather(
-        grid, [key[None], value[None], w_out[None], w_in[None], w_back[None]],
-        [(0, "zy", None), (1, "zy", None), (2, "zyx", None), (3, "zyx", None), (4, "zxy", None)], "gather_rest", 1)
-    key_all, value_all = key_all.reshape(slots, width), value_all.reshape(slots, width)
-    out_full, in_full, back_full = out_all.reshape(width, width), in_all.reshape(width, hidden_size), back_all.reshape(hidden_size, width)
+    whole = grid.depth <= 4 and part % 8 == 0 and part_ff <= 128
+    if whole:
+        vec_block = jnp.pad(vectors, ((0, 0), (0, 120)))
+        bias_block = jnp.pad(ffn_bias[None], ((0, 7), (0, 128 - part_ff)))[None]
+        qkv_full, vec_all, bias_all, out_all, in_all, back_all, key_all, value_all, query_scaled = fetch(
+            grid, rows_in, w_qkv, vec_block, bias_block, w_out[None], w_in[None], w_back[None], scale)
+        vec = vec_all[:, :8].T.astype(f4)
+        ffn_full = bias_all[:, 0, :part_ff].reshape(1, hidden_size).astype(f4)
+        out_full, in_full, back_full = out_all.reshape(width, width), in_all.reshape(width, hidden_size), back_all.reshape(hidden_size, width)
+    else:
+        everywhere = lambda a: lax.all_gather(a, ("seq", "ctx"), axis=0, tiled=True)
+        qkv_full, out_full, in_full, back_full = everywhere(w_qkv), everywhere(w_out), everywhere(w_in), everywhere(w_back)
+        vec = everywhere(vectors).T.astype(f4)
+        ffn_full = everywhere(ffn_bias)[None].astype(f4)
+        projected = jnp.dot(rows_in, qkv_full, preferred_element_type=f4)
+        query_scaled = (projected[:, :width] + vec[0]).astype(bf) * jnp.asarray(scale, bf)
+        key = projected[:, width:2 * width].astype(bf)
+        value = (projected[:, 2 * width:] + vec[1]).astype(bf)
+        key_all, value_all = (lax.all_gather(a, "ctx", axis=0, tiled=True) for a in (key, value))
 
     tile = min(slots, 2048)
-    query_scaled = query * jnp.asarray(scale, bf)
     attended_f, lse = attend(query_scaled, key_all, value_all, lengths, HEADS, tile)
     attended = attended_f.astype(bf)
     branch = jnp.dot(attended, out_full, preferred_element_type=f4) + vec[2]
@@ -528,27 +647,28 @@
 
     def outer(a, b):
         return lax.dot_general(a, b, (((0,), (0,)), ((), ())), preferred_element_type=f4).astype(bf)
-    g_back = outer(active, grad_second_low).reshape(devices, part_ff, width)
-    g_in = outer(first_low, grad_hidden).reshape(devices, part, hidden_size)
-    g_out = outer(attended, grad_branch).reshape(devices, part, width)
-    grad_query, g_key, g_value = attend_back(query_scaled, key_all, value_all, grad_attended, attended_f, lse, lengths, HEADS, tile)
-    own_key, own_value, d_out, d_in, d_back = reduce_blocks(
-        grid, [g_key.reshape(grid.ctx, rows, width), g_value.reshape(grid.ctx, rows, width), g_out, g_in, g_back],
-        ["zy", "zy", "zyx", "zyx", "zxy"], "reduce_rest", 2)
-    grad_projected = jnp.concatenate((grad_query, own_key[0].astype(bf), own_value[0].astype(bf)), axis=1)
-    g_qkv = outer(rows_in, grad_projected).reshape(devices, part, 3 * width)
+    g_back = outer(active, grad_second_low)
+    g_in = outer(first_low, grad_hidden)
+    g_out = outer(attended, grad_branch)
+    grad_ffn = jnp.sum(grad_hidden.astype(f4), axis=0)
+    sums = (jnp.sum(grad_branch.astype(f4), axis=0), jnp.sum(grad_first * norm_one, axis=0), jnp.sum(grad_first, axis=0),
+            jnp.sum(grad_second_low.astype(f4), axis=0), jnp.sum(grad_result * norm_two, axis=0), jnp.sum(grad_result, axis=0))
+    if whole:
+        g_vec = jnp.pad(jnp.stack(sums).T, ((0, 0), (2, 120)))
+        g_bias = jnp.pad(grad_ffn.reshape(devices, 1, part_ff), ((0, 0), (0, 7), (0, 128 - part_ff)))
+        d_qkv, d_out, d_in, d_back, d_bias, d_vec, grad_inputs = settle(
+            grid, width // HEADS, lengths, key_all, value_all, g_out.reshape(devices, part, width), g_in.reshape(devices, part, hidden_size),
+            g_back.reshape(devices, part_ff, width), qkv_full, query_scaled, grad_attended, attended_f, lse, rows_in, grad_branch_full, g_bias, g_vec)
+        return (result[None], grad_inputs[None], d_qkv[0], d_out[0], d_in[0], d_back[0], d_vec[0, :, :8], d_bias[0, 0, :part_ff])
+    grad_query, g_key, g_value, sum_value = attend_back(query_scaled, key_all, value_all, grad_attended, attended_f, lse, lengths, HEADS, tile)
+    sums = jnp.stack((jnp.sum(grad_query.astype(f4), axis=0), sum_value.reshape(width)) + sums)
+    home = lambda a, axes: lax.psum_scatter(a.astype(f4), axes, scatter_dimension=0, tiled=True)
+    own_key, own_value = (home(a, "ctx").astype(bf) for a in (g_key, g_value))
+    grad_projected = jnp.concatenate((grad_query, own_key, own_value), axis=1)
     grad_inputs = grad_branch_full + lax.dot_general(grad_projected, qkv_full, (((1,), (1,)), ((), ())), preferred_element_type=f4)
-    sums = jnp.stack((
-        jnp.sum(grad_query.astype(f4), axis=0), jnp.sum(own_value[0].astype(bf).astype(f4), axis=0),
-        jnp.sum(grad_branch.astype(f4), axis=0), jnp.sum(grad_first * norm_one, axis=0), jnp.sum(grad_first, axis=0),
-        jnp.sum(grad_second_low.astype(f4), axis=0), jnp.sum(grad_result * norm_two, axis=0), jnp.sum(grad_result, axis=0)))
-    grad_ffn = jnp.sum(grad_hidden.astype(f4), axis=0)
-    blocks = jnp.pad(sums.reshape(8, devices, part).transpose(1, 0, 2), ((0, 0), (0, 0), (0, 128 - part)))
-    ffn_blocks = jnp.pad(grad_ffn.reshape(devices, 1, part_ff), ((0, 0), (0, 7), (0, 128 - part_ff)))
-    g_small = jnp.concatenate((blocks, ffn_blocks), axis=1)
-    d_qkv_a, d_qkv_b, d_small = reduce_blocks(grid, [g_qkv[:, :, :half], g_qkv[:, :, half:], g_small], ["zyx", "zxy", "zyx"], "reduce_qkv", 3)
-    d_qkv = jnp.concatenate((d_qkv_a[0], d_qkv_b[0]), axis=1)
-    return (result[None], grad_inputs[None], d_qkv, d_out[0], d_in[0], d_back[0], d_small[0, :8, :part].T, d_small[0, 8, :part_ff])
+    both = ("seq", "ctx")
+    return (result[None], grad_inputs[None], home(outer(rows_in, grad_projected), both), home(g_out, both), home(g_in, both), home(g_back, both),
+            home(sums.T, both), home(grad_ffn, both))
 
 def solution(mesh):
     grid = Grid(mesh.shape["seq"], mesh.shape["ctx"])

time: 333 us -> 255 us (0.77)
  Pallas kernels: 278 us -> 206 us
  local copies, waits for them, and re-layouts: 9.09 us -> 20.7 us
  other arithmetic: 13.8 us -> 3.65 us
  matrix products: 29.7 us -> 22.4 us
    pallas_call x5 -> x2, Pallas kernels: 269 us -> 197 us  [the longest x1 106 us: settle(): pl.pallas_call(functools.partial(settle_kernel, grid, size), out_shape=[S...]
    dot_general x2 -> x0, matrix products: 5.79 us -> none  [the longest x1 3.02 us: per_device(): lax.dot_general(grad_projected, qkv_full, (((1,), (1,)), ((), ())), prefe...]
    unnamed x55 -> x37, local copies, waits for them, and re-layouts: 2.57 us -> 7.84 us
    another operation x9 -> x8, local copies, waits for them, and re-layouts: 0.83 us -> 5.25 us  [per_device(): g_vec = jnp.pad(jnp.stack(sums).T, ((0, 0), (2, 120)))]
    dot_general x4 -> x3, matrix products: 9.86 us -> 8.79 us  [outer(): lax.dot_general(a, b, (((0,), (0,)), ((), ())), preferred_element_type=f4)]
where the time goes in v3:
time: 255 us; the launch traced here: 254 us
  Pallas kernels  206 us (81%)
  matrix products  22.4 us (9%)
  local copies, waits for them, and re-layouts  20.7 us (8%)
  other arithmetic  3.65 us (1%)
    pallas_call x1, Pallas kernels, settle(): pl.pallas_call(functools.partial(settle_kernel, grid, size), out_shape=[S...  106 us
    pallas_call x1, Pallas kernels, fetch(): pl.pallas_call(functools.partial(fetch_kernel, grid, scale), out_shape=[f...  91.4 us
    pallas_call x1, Pallas kernels, attend(): pl.pallas_call(functools.partial(forward_kernel, size, tiles), grid_spec=...  9.25 us
    dot_general x3, matrix products, outer(): lax.dot_general(a, b, (((0,), (0,)), ((), ())), preferred_element_type=f4)  8.79 us
    unnamed x37, local copies, waits for them, and re-layouts  7.84 us
    another operation x8, local copies, waits for them, and re-layouts, per_device(): g_vec = jnp.pad(jnp.stack(sums).T, ((0, 0), (2, 120)))  5.25 us

profile of v3, /device:TPU:0, one launch (start us, length us, event | category | flops | bytes accessed | tf_op | source)
XLA Modules:
  0.0 254.4 jit_solution(9687709685187408274)
XLA Ops:
  1.3 1.2 pad_bitcast_fusion.refs_3_
  2.5 0.8 copy.27
  3.3 0.6 pad.16.refs_2_
  3.9 91.4 %fetch.1 = (bf16[768,2304]{1,0:T(8,128)(2,1)}, bf16[768,128]{1,0:T(8,128)(2,1)}, bf16[32,8,128]{2,1,0:T(8,128)(2,1)}, bf16[32,24,768]{2,1,0:T(8,128)(2,1)}, bf16...) custom-call(bf16[128,768]{1,0:T(8,128)(2,1)} %bitcast.59, ...), custom_call_target="tpu_custom_call" | custom-call | tf_op jit(solution)/shard_map/fetch/pallas_call | solution.py:207
  95.3 0.9 convert_reduce_fusion.3
  96.2 1.0 convert_bitcast_fusion
  97.2 1.3 slice_reduce_fusion.1
  98.5 9.3 %attend.1 = (f32[128,768]{1,0:T(8,128)}, f32[6,1,256]{2,1,0:T(1,128)}) custom-call(s32[1]{0:T(128)} %copy.35.len_ref.refs_0_, bf16[128,768]{1,0:T(8,128)(2,1)} %get-tuple-element.26.q_ref.refs_7_, bf16[2048,768]{1,0:T(8,128)(2,1)} %get-tuple-element.27.k_ref.refs_1_, bf16[2048,768]{1,0:T(8,128)(2,1)} %get-tuple-element.28.v_ref.refs_2_), custom_call_target="tpu_custom_call" | custom-call | tf_op jit(solution)/shard_map/attend/pallas_call | solution.py:398
  107.8 1.4 fusion.28
  109.4 3.3 %convolution_add_fusion = f32[128,3072]{1,0:T(8,128)S(1)} fusion(bf16[768,3072]{1,0:T(8,128)(2,1)} %bitcast.48, f32[3072]{0:T(1024)S(1)} %reshape.101, f32[128,768]{1,0:T(8,128)S(1)} %get-tuple-element.88, f32[768]{0:T(1024)S(1)} %get-tuple-element.77, f32[768]{0:T(1024)S(1)} %get-tuple-element.78, f32[128]{0:T(128)S(1)} %add_rsqrt_fusion.1, ...), kind=kOutput, calls=%fused_computation.3 | convolution fusion | flops 604864512 | bytes 6704128 | tf_op jit(solution)/shard_map/dot_general | solution.py:630
  112.8 3.4 %fusion.29 = (f32[128]{0:T(128)S(1)}, f32[128,768]{1,0:T(8,128)S(1)}) fusion(f32[768]{0:T(1024)S(1)} %get-tuple-element.76, bf16[3072,768]{1,0:T(8,128)(2,1)} %bitcast.53, f32[128,3072]{1,0:T(8,128)S(1)} %convolution_add_fusion, f32[768]{0:T(1024)S(1)} %get-tuple-element.77, f32[768]{0:T(1024)S(1)} %get-tuple-element.78, f32[128]{0:T(128)S(1)} %add_rsqrt_fusion.1, ...), kind=kOutput, calls=%fused_computation.72 | convolution fusion | flops 606633856 | bytes 7088640 | tf_op jit(solution)/shard_map/dot_general | solution.py:633
  117.9 0.9 convert_reduce_fusion.1
  118.8 2.4 convert_reduce_fusion
  121.2 1.8 multiply_reduce_fusion
  125.0 1.2 convolution_convert_fusion.3.refs_8_
  126.2 0.8 reshape.100
  127.1 1.4 stack.27
  128.5 0.7 pad.18.refs_13_
  129.1 1.0 copy.28
  130.1 0.9 pad.19.refs_14_
  131.0 1.5 convolution_convert_fusion.2
  132.6 3.6 %convolution_convert_fusion = bf16[3072,768]{1,0:T(8,128)(2,1)} fusion(f32[128,768]{1,0:T(8,128)S(1)} %copy-done.3, f32[128,3072]{1,0:T(8,128)S(1)} %convolution_add_fusion), kind=kOutput, calls=%fused_computation | convolution fusion | flops 608403456 | bytes 6684672 | tf_op jit(solution)/shard_map/dot_general | solution.py:649
  136.1 3.7 %convolution_convert_fusion.1 = bf16[768,3072]{1,0:T(8,128)(2,1)} fusion(bf16[128,3072]{1,0:T(8,128)(2,1)S(1)} %copy-done.6, f32[128,768]{1,0:T(8,128)S(1)} %get-tuple-element.88, f32[768]{0:T(1024)S(1)} %get-tuple-element.77, f32[768]{0:T(1024)S(1)} %get-tuple-element.78, f32[128]{0:T(128)S(1)} %add_rsqrt_fusion.1, f32[128]{0:T(128)S(1)} %broadcast_multiply_fusion.5), kind=kOutput, calls=%fused_computation.1 | convolution fusion | flops 606830592 | bytes 5905408 | tf_op jit(solution)/shard_map/dot_general | solution.py:649
  139.8 105.6 %settle.1 = (f32[1,24,2304]{2,1,0:T(8,128)}, f32[1,24,768]{2,1,0:T(8,128)}, f32[1,24,3072]{2,1,0:T(8,128)}, f32[1,96,768]{2,1,0:T(8,128)}, f32[1,8,128]{2,1,0:T(...) custom-call(s32[1]{0:T(128)} %copy.35.len_ref.refs_0_, bf16[2048,768]{1,0:T(8,128)(2,1)} %get-tuple-element.27.k_ref.refs_1_, ...), custom_call_target="tpu_custom_call" | custom-call | tf_op jit(solution)/shard_map/settle/pallas_call | solution.py:566
  245.4 1.3 slice_bitcast_fusion.1
  246.7 0.7 slice_bitcast_fusion
  247.4 0.7 copy.29
  248.1 1.8 copy.36
  249.8 1.6 copy.37
  251.5 1.5 copy.38
  253.0 0.7 copy.39
  253.7 0.7 copy.40
  (51 shorter events, 4.0 us)
Async XLA Ops:
  98.5 9.3 %copy-start.1 = (bf16[32,24,768]{2,1,0:T(8,128)(2,1)S(1)}, bf16[32,24,768]{2,1,0:T(8,128)(2,1)}, u32[]{:S(2)}) copy-start(bf16[32,24,768]{2,1,0:T(8,128)(2,1)} %get-tuple-element.30) | copy-start | bytes 3538948
  98.5 9.3 %copy-start.7 = (bf16[1,128,768]{2,1,0:T(8,128)(2,1)S(1)}, bf16[1,128,768]{2,1,0:T(8,128)(2,1)}, u32[]{:S(2)}) copy-start(bf16[1,128,768]{2,1,0:T(8,128)(2,1)} %param.9) | copy-start | bytes 589828
  109.4 9.4 %slice-start.2 = ((s8[4718592]{0:T(1024)(128)(4,1)}), s8[4194304]{0:T(1024)(128)(4,1)S(1)}, s32[]{:S(2)}) async-start(s8[4718592]{0:T(1024)(128)(4,1)} %bitcast.54), calls=%async_computation.2 | async-start | bytes 8388608
  112.8 3.6 %copy-start.8 = (bf16[1,128,768]{2,1,0:T(8,128)(2,1)S(1)}, bf16[1,128,768]{2,1,0:T(8,128)(2,1)}, u32[]{:S(2)}) copy-start(bf16[1,128,768]{2,1,0:T(8,128)(2,1)} %param.11) | copy-start | bytes 589828
  112.8 6.0 %slice-start.3 = ((s8[4718592]{0:T(1024)(128)(4,1)}), s8[524288]{0:T(1024)(128)(4,1)S(1)}, s32[]{:S(2)}) async-start(s8[4718592]{0:T(1024)(128)(4,1)} %bitcast.54), calls=%async_computation.3 | async-start | bytes 1048576
  117.9 3.3 %slice-start = ((s8[4718592]{0:T(1024)(128)(4,1)}), s8[4194304]{0:T(1024)(128)(4,1)S(1)}, s32[]{:S(2)}) async-start(s8[4718592]{0:T(1024)(128)(4,1)} %bitcast.49), calls=%async_computation | async-start | bytes 8388608
  118.8 2.4 copy-start.2
  118.8 2.4 slice-start.1
  121.2 1.9 copy-start.5
  125.0 6.0 %copy-start = (f32[128,768]{1,0:T(8,128)}, f32[128,768]{1,0:T(8,128)S(1)}, u32[]{:S(2)}) copy-start(f32[128,768]{1,0:T(8,128)S(1)} %get-tuple-element.85.refs_12_) | copy-start | bytes 1179652
  126.2 4.8 %copy-start.4 = (f32[128,768]{1,0:T(8,128)S(1)}, f32[128,768]{1,0:T(8,128)}, u32[]{:S(2)}) copy-start(f32[128,768]{1,0:T(8,128)} %get-tuple-element.29.refs_9_) | copy-start | bytes 1179652
  129.1 3.4 %copy-start.3 = (f32[128,768]{1,0:T(8,128)S(1)}, f32[128,768]{1,0:T(8,128)}, u32[]{:S(2)}) copy-start(f32[128,768]{1,0:T(8,128)} %copy-done.2) | copy-start | bytes 1179652
  132.6 3.6 %copy-start.6 = (bf16[128,3072]{1,0:T(8,128)(2,1)S(1)}, bf16[128,3072]{1,0:T(8,128)(2,1)}, u32[]{:S(2)}) copy-start(bf16[128,3072]{1,0:T(8,128)(2,1)} %copy-done.5) | copy-start | bytes 2359300
  245.4 7.6 %copy-start.10 = (f32[1,24,3072]{2,1,0:T(8,128)S(1)}, f32[1,24,3072]{2,1,0:T(8,128)}, u32[]{:S(2)}) copy-start(f32[1,24,3072]{2,1,0:T(8,128)} %get-tuple-element.40) | copy-start | bytes 884740
  245.4 8.3 %copy-start.9 = (f32[1,96,768]{2,1,0:T(8,128)S(1)}, f32[1,96,768]{2,1,0:T(8,128)}, u32[]{:S(2)}) copy-start(f32[1,96,768]{2,1,0:T(8,128)} %get-tuple-element.41) | copy-start | bytes 884740

commit v4 on v3

--- a/solution.py
+++ b/solution.py
@@ -589,6 +589,101 @@
     slope = cdf + v * jnp.exp(-0.5 * v * v) * ((2 * jnp.pi) ** -0.5)
     return v * cdf, slope
 
+def layer_kernel(grid, length, w_out_hbm, w_in_hbm, w_back_hbm, attended_ref, x, cotangent, vec_all, bias_all,
+                 g_out_hbm, g_in_hbm, g_back_hbm, result, grad_attended, base, g_bias, g_vec,
+                 w_out, w_in, w_back, g_out, g_in, g_back, bias, in_sem, out_sem):
+    bf = jnp.bfloat16
+    loads = [pltpu.make_async_copy(src, dst, in_sem.at[n]) for n, (src, dst) in enumerate(((w_out_hbm, w_out), (w_in_hbm, w_in), (w_back_hbm, w_back)))]
+    for copy in loads: copy.start()
+    stores = [pltpu.make_async_copy(src, dst, out_sem.at[n]) for n, (src, dst) in enumerate(((g_out, g_out_hbm), (g_in, g_in_hbm), (g_back, g_back_hbm)))]
+    rows, width = x.shape
+    devices, part_ff = g_back.shape[:2]
+    part = g_in.shape[1]
+    lane = lax.broadcasted_iota(jnp.int32, (16, 128), 1)
+    pick = (lane == lax.broadcasted_iota(jnp.int32, (16, 128), 0)).astype(bf)
+    vec = nt(pick, vec_all[...])
+    for k in range(devices):
+        bias[0:1, k * part_ff:(k + 1) * part_ff] = f32(bias_all[k])[0:1, :part_ff]
+    attended = attended_ref[...].astype(bf)
+    loads[0].wait()
+    branch = nn(attended, w_out[...]) + vec[2:3]
+    norm_one, r_one = normalize(f32(x[...]) + branch)
+    first = norm_one * vec[3:4] + vec[4:5]
+    first_low = first.astype(bf)
+    loads[1].wait()
+    hidden = nn(first_low, w_in[...]) + bias[0:1]
+    active_f, slope = gelu_parts(hidden)
+    active = active_f.astype(bf)
+    loads[2].wait()
+    second = nn(active, w_back[...]) + vec[5:6]
+    norm_two, r_two = normalize(first + second)
+    result[...] = (norm_two * vec[6:7] + vec[7:8]).astype(bf)
+    slot = lax.broadcasted_iota(jnp.int32, (rows, 1), 0) + lax.axis_index("ctx") * rows
+    grad_result = jnp.where(slot < length[0], f32(cotangent[...]), 0.0)
+    grad_second = normalize_back(grad_result, norm_two, r_two, vec[6:7])
+    grad_second_low = grad_second.astype(bf)
+    grad_hidden_f = nt(grad_second_low, w_back[...]) * slope
+    grad_hidden = grad_hidden_f.astype(bf)
+    for n in range(devices * part_ff // width):
+        full = tn(active[:, n * width:(n + 1) * width], grad_second_low).astype(bf)
+        for k in range(width // part_ff):
+            g_back[n * (width // part_ff) + k] = full[k * part_ff:(k + 1) * part_ff]
+    stores[2].start()
+    for n in range(devices * part_ff // width):
+        full = tn(first_low, grad_hidden[:, n * width:(n + 1) * width])
+        for k in range(devices):
+            g_in[k, :, n * width:(n + 1) * width] = full[k * part:(k + 1) * part].astype(bf)
+    stores[1].start()
+    grad_first = grad_second + nt(grad_hidden, w_in[...])
+    grad_branch_full = normalize_back(grad_first, norm_one, r_one, vec[3:4])
+    base[...] = grad_branch_full
+    grad_branch = grad_branch_full.astype(bf)
+    grad_attended[...] = nt(grad_branch, w_out[...]).astype(bf)
+    full = tn(attended, grad_branch)
+    for k in range(devices):
+        g_out[k] = full[k * part:(k + 1) * part].astype(bf)
+    stores[0].start()
+    total = lambda a: jnp.sum(f32(a), axis=0, keepdims=True)
+    sums = total(grad_hidden)
+    g_bias[...] = jnp.zeros_like(g_bias)
+    for k in range(devices):
+        g_bias[k, 0:1, 0:part_ff] = sums[:, k * part_ff:(k + 1) * part_ff]
+    stack = jnp.concatenate((jnp.zeros((2, width), jnp.float32), total(grad_branch), total(grad_first * norm_one), total(grad_first),
+                             total(grad_second_low), total(grad_result * norm_two), total(grad_result), jnp.zeros((120, width), jnp.float32)), axis=0)
+    for n in range(width // 128):
+        g_vec[n * 128:(n + 1) * 128, :] = jnp.transpose(stack[:, n * 128:(n + 1) * 128])
+    for copy in stores: copy.wait()
+
+def layer(grid, length, w_out, w_in, w_back, attended, x, cotangent, vec_all, bias_all):
+    bf, f4 = jnp.bfloat16, jnp.float32
+    rows, width = x.shape
+    hidden = w_in.shape[1]
+    devices = grid.seqs * grid.ctx
+    S, M, D = jax.ShapeDtypeStruct, pltpu.VMEM, pltpu.SemaphoreType.DMA
+    V, A = pl.BlockSpec(memory_space=pltpu.VMEM), pl.BlockSpec(memory_space=pl.ANY)
+    grads = [(devices, width // devices, width), (devices, width // devices, hidden), (devices, hidden // devices, width)]
+    return pl.pallas_call(
+        functools.partial(layer_kernel, grid),
+        out_shape=[S(g, bf) for g in grads] + [S((rows, width), bf), S((rows, width), bf), S((rows, width), f4), S((devices, 8, 128), f4), S((width, 128), f4)],
+        in_specs=[pl.BlockSpec(memory_space=pltpu.SMEM)] + [A] * 3 + [V] * 5, out_specs=[A] * 3 + [V] * 5,
+        scratch_shapes=[M(w.shape, bf) for w in (w_out, w_in, w_back)] + [M(g, bf) for g in grads] + [M((8, hidden), f4), D((3,)), D((3,))],
+        compiler_params=pltpu.CompilerParams(vmem_limit_bytes=60 * 2**20),
+        name="layer",
+    )(length, w_out, w_in, w_back, attended, x, cotangent, vec_all, bias_all)
+
+def deliver_kernel(*refs):
+    n = len(refs) // 2
+    for src, dst in zip(refs[:n], refs[n:]):
+        if len(dst.shape) == 3: dst[0] = src[...]
+        else: dst[...] = src[0, :dst.shape[0], :dst.shape[1]]
+
+def deliver(arrays, shapes):
+    V = pl.BlockSpec(memory_space=pltpu.VMEM)
+    return pl.pallas_call(
+        deliver_kernel, out_shape=[jax.ShapeDtypeStruct(s, jnp.float32) for s in shapes],
+        in_specs=[V] * len(arrays), out_specs=[V] * len(arrays), name="deliver",
+    )(*arrays)
+
 def per_device(grid, inputs, lengths, cotangent, w_qkv, w_out, w_in, w_back, vectors, ffn_bias):
     bf, f4 = jnp.bfloat16, jnp.float32
     rows_in = inputs[0]
@@ -606,8 +701,6 @@
         bias_block = jnp.pad(ffn_bias[None], ((0, 7), (0, 128 - part_ff)))[None]
         qkv_full, vec_all, bias_all, out_all, in_all, back_all, key_all, value_all, query_scaled = fetch(
             grid, rows_in, w_qkv, vec_block, bias_block, w_out[None], w_in[None], w_back[None], scale)
-        vec = vec_all[:, :8].T.astype(f4)
-        ffn_full = bias_all[:, 0, :part_ff].reshape(1, hidden_size).astype(f4)
         out_full, in_full, back_full = out_all.reshape(width, width), in_all.reshape(width, hidden_size), back_all.reshape(hidden_size, width)
     else:
         everywhere = lambda a: lax.all_gather(a, ("seq", "ctx"), axis=0, tiled=True)
@@ -622,6 +715,15 @@
 
     tile = min(slots, 2048)
     attended_f, lse = attend(query_scaled, key_all, value_all, lengths, HEADS, tile)
+    if whole:
+        g_out, g_in, g_back, result, grad_attended, base, g_bias, g_vec = layer(
+            grid, lengths, out_full, in_full, back_full, attended_f, rows_in, cotangent[0], vec_all, bias_all)
+        d_qkv, d_out, d_in, d_back, d_bias, d_vec, grad_inputs = settle(
+            grid, width // HEADS, lengths, key_all, value_all, g_out, g_in, g_back, qkv_full, query_scaled, grad_attended, attended_f, lse, rows_in, base, g_bias, g_vec)
+        grad_inputs, d_qkv, d_out, d_in, d_back, d_vec, d_bias = deliver(
+            (grad_inputs, d_qkv, d_out, d_in, d_back, d_vec, d_bias),
+            ((1, rows, width), (part, 3 * width), (part, width), (part, hidden_size), (part_ff, width), (part, 8), (1, part_ff)))
+        return (result[None], grad_inputs, d_qkv, d_out, d_in, d_back, d_vec, d_bias[0])
     attended = attended_f.astype(bf)
     branch = jnp.dot(attended, out_full, preferred_element_type=f4) + vec[2]
     norm_one, r_one = normalize(rows_in.astype(f4) + branch)
@@ -653,13 +755,6 @@
     grad_ffn = jnp.sum(grad_hidden.astype(f4), axis=0)
     sums = (jnp.sum(grad_branch.astype(f4), axis=0), jnp.sum(grad_first * norm_one, axis=0), jnp.sum(grad_first, axis=0),
             jnp.sum(grad_second_low.astype(f4), axis=0), jnp.sum(grad_result * norm_two, axis=0), jnp.sum(grad_result, axis=0))
-    if whole:
-        g_vec = jnp.pad(jnp.stack(sums).T, ((0, 0), (2, 120)))
-        g_bias = jnp.pad(grad_ffn.reshape(devices, 1, part_ff), ((0, 0), (0, 7), (0, 128 - part_ff)))
-        d_qkv, d_out, d_in, d_back, d_bias, d_vec, grad_inputs = settle(
-            grid, width // HEADS, lengths, key_all, value_all, g_out.reshape(devices, part, width), g_in.reshape(devices, part, hidden_size),
-            g_back.reshape(devices, part_ff, width), qkv_full, query_scaled, grad_attended, attended_f, lse, rows_in, grad_branch_full, g_bias, g_vec)
-        return (result[None], grad_inputs[None], d_qkv[0], d_out[0], d_in[0], d_back[0], d_vec[0, :, :8], d_bias[0, 0, :part_ff])
     grad_query, g_key, g_value, sum_value = attend_back(query_scaled, key_all, value_all, grad_attended, attended_f, lse, lengths, HEADS, tile)
     sums = jnp.stack((jnp.sum(grad_query.astype(f4), axis=0), sum_value.reshape(width)) + sums)
     home = lambda a, axes: lax.psum_scatter(a.astype(f4), axes, scatter_dimension=0, tiled=True)

time: 255 us -> 232 us (0.910)
  matrix products: 22.4 us -> 0 us
  Pallas kernels: 206 us -> 226 us
  local copies, waits for them, and re-layouts: 20.7 us -> 3.97 us
  other arithmetic: 3.65 us -> 0 us
    dot_general x9 -> x0, matrix products: 22.4 us -> none  [the longest x3 8.79 us: outer(): lax.dot_general(a, b, (((0,), (0,)), ((), ())), preferred_element_type=f4)]
    pallas_call x0 -> x2, Pallas kernels: none -> 19.8 us  [the longest x1 17.4 us: layer(): pl.pallas_call(functools.partial(layer_kernel, grid), out_shape=[S(g, bf)...]
    unnamed x37 -> x2, local copies, waits for them, and re-layouts: 7.84 us -> 2.13 us
    another operation x8 -> x0, local copies, waits for them, and re-layouts: 5.25 us -> none  [per_device(): g_vec = jnp.pad(jnp.stack(sums).T, ((0, 0), (2, 120)))]
where the time goes in v4:
time: 232 us; the launch traced here: 231 us
  Pallas kernels  226 us (97%)
  local copies, waits for them, and re-layouts  3.97 us (2%)
    pallas_call x1, Pallas kernels, settle(): pl.pallas_call(functools.partial(settle_kernel, grid, size), out_shape=[S...  106 us
    pallas_call x1, Pallas kernels, fetch(): pl.pallas_call(functools.partial(fetch_kernel, grid, scale), out_shape=[f...  91.4 us
    pallas_call x1, Pallas kernels, layer(): pl.pallas_call(functools.partial(layer_kernel, grid), out_shape=[S(g, bf)...  17.4 us
    pallas_call x1, Pallas kernels, attend(): pl.pallas_call(functools.partial(forward_kernel, size, tiles), grid_spec=...  9.15 us

profile of v4, /device:TPU:0, one launch (start us, length us, event | category | flops | bytes accessed | tf_op | source)
XLA Modules:
  0.0 231.3 jit_solution(5037859642856668594)
XLA Ops:
  1.3 1.2 pad_bitcast_fusion.refs_3_
  2.5 0.8 copy.17
  3.3 0.6 pad.8.refs_2_
  3.9 91.4 %fetch.1 = (bf16[768,2304]{1,0:T(8,128)(2,1)}, bf16[768,128]{1,0:T(8,128)(2,1)}, bf16[32,8,128]{2,1,0:T(8,128)(2,1)}, bf16[32,24,768]{2,1,0:T(8,128)(2,1)}, bf16...) custom-call(bf16[128,768]{1,0:T(8,128)(2,1)} %bitcast.15, ...), custom_call_target="tpu_custom_call" | custom-call | tf_op jit(solution)/shard_map/fetch/pallas_call | solution.py:207
  95.3 9.1 %attend.1 = (f32[128,768]{1,0:T(8,128)}, f32[6,1,256]{2,1,0:T(1,128)}) custom-call(s32[1]{0:T(128)S(6)} %copy.19.len_ref.length.refs_0_, bf16[128,768]{1,0:T(8,128)(2,1)} %get-tuple-element.44.q_ref.refs_7_, bf16[2048,768]{1,0:T(8,128)(2,1)} %get-tuple-element.45.k_ref.refs_1_, bf16[2048,768]{1,0:T(8,128)(2,1)} %get-tuple-element.46.v_ref.refs_2_), custom_call_target="tpu_custom_call" | custom-call | tf_op jit(solution)/shard_map/attend/pallas_call | solution.py:398
  104.4 17.4 %layer.1 = (bf16[32,24,768]{2,1,0:T(8,128)(2,1)}, bf16[32,24,3072]{2,1,0:T(8,128)(2,1)}, bf16[32,96,768]{2,1,0:T(8,128)(2,1)}, bf16[128,768]{1,0:T(8,128)(2,1)},...) custom-call(s32[1]{0:T(128)S(6)} %copy.19.len_ref.length.refs_0_, ...), custom_call_target="tpu_custom_call" | custom-call | tf_op jit(solution)/shard_map/layer/pallas_call | solution.py:665
  121.8 105.6 %settle.1 = (f32[1,24,2304]{2,1,0:T(8,128)}, f32[1,24,768]{2,1,0:T(8,128)}, f32[1,24,3072]{2,1,0:T(8,128)}, f32[1,96,768]{2,1,0:T(8,128)}, f32[1,8,128]{2,1,0:T(...) custom-call(s32[1]{0:T(128)S(6)} %copy.19.len_ref.length.refs_0_, bf16[2048,768]{1,0:T(8,128)(2,1)} %get-tuple-element.45.k_ref.refs_1_, ...), custom_call_target="tpu_custom_call" | custom-call | tf_op jit(solution)/shard_map/settle/pallas_call | solution.py:566
  227.5 2.4 %deliver.1 = (f32[1,128,768]{2,1,0:T(8,128)}, f32[24,2304]{1,0:T(8,128)}, f32[24,768]{1,0:T(8,128)}, f32[24,3072]{1,0:T(8,128)}, f32[96,768]{1,0:T(8,128)}, /*index=5*/f32[24,8]{1,0:T(8,128)}, f32[1,96]{1,0:T(1,128)}) custom-call(f32[128,768]{1,0:T(8,128)} %get-tuple-element.60.refs_0_, f32[1,24,2304]{2,1,0:T(8,128)} %get-tuple-element.61.refs_1_, ...), custom_call_target="tpu_custom_call" | custom-call | tf_op jit(solution)/shard_map/deliver/pallas_call | solution.py:682
  229.9 1.4 copy.18

commit v5 on v4

--- a/solution.py
+++ b/solution.py
@@ -49,7 +49,8 @@
         self.send, self.zsend, self.recv, self.local = sems
         self.order, self.cols = order, cols
         self.s, self.z, self.y, self.c = grid.here()
-        self.rest = order[1:]
+        self.early = order[0] == 'y'
+        self.rest = 'x' if self.early else order[1:]
     def rows(self, start, n):
         if len(self.dst.shape) == 3:
             return self.dst.at[start] if n is None else self.dst.at[pl.ds(start, n)]
@@ -76,16 +77,18 @@
         y = 1 - self.y if 'y' in flips else self.y
         c = 1 - self.c if 'c' in flips else self.c
         return cid(z, y, c) + (s * self.g.ctx if 'x' in self.order else 0)
-    def zpush(self, src, b, z, side):
+    def zpush(self, src, b, z, side, f=''):
         ok = self.z < self.g.depth - 1 if side == '+' else self.z > 0
         @pl.when(ok)
         def _():
-            self.push(src, b, self.dev(side), self.zsend.at[0 if side == '+' else 1, z])
-    def start(self, dims=None):
+            self.push(src, b, self.dev(side), self.zsend.at[0 if side == '+' else 1, z + (self.g.depth if f else 0)])
+    def start(self):
         own = self.at('', self.z)
+        if self.early:
+            self.push(self.own(), own, self.dev('y'), self.send)
         for side in '+-':
             self.zpush(self.own(), own, self.z, side)
-        for dim in dims or self.rest + 'c':
+        for dim in self.rest + 'c':
             self.push(self.own(), own, self.dev(dim), self.send)
         pltpu.make_async_copy(self.own(), self.view(own), self.local).start()
     def sides(self, d, body):
@@ -98,18 +101,15 @@
         @pl.when(self.z + d < self.g.depth)
         def _():
             body(self.z + d, '+')
-    def line(self, d, dims=None):
+    def line(self, d, f=''):
         def go(z, side):
-            b = self.at('', z)
+            b = self.at(f, z)
             self.wait(b)
-            self.zpush(self.view(b), b, z, '+' if side == '-' else '-')
-            for k in dims or self.rest + 'c':
+            for way in '+-':
+                if way != side:
+                    self.zpush(self.view(b), b, z, way, f)
+            for k in self.rest + 'c':
                 self.push(self.view(b), b, self.dev(k), self.send)
-        self.sides(d, go)
-    def late(self, dim, d):
-        def go(z, side):
-            b = self.at('', z)
-            self.push(self.own() if side == '' else self.view(b), b, self.dev(dim), self.send)
         self.sides(d, go)
     def cross(self, flips, dims, d):
         def go(z, side):
@@ -120,6 +120,15 @@
         self.sides(d, go)
     def step(self, t):
         r = self.rest
+        if self.early:
+            if t < self.g.depth:
+                self.line(t)
+            if t <= self.g.depth:
+                self.line(t - 1, 'y')
+                self.cross('x', 'c', t - 1)
+            if 2 <= t <= self.g.depth + 1:
+                self.cross('yx', 'c', t - 2)
+            return
         if t < self.g.depth:
             self.line(t)
         if 1 <= t <= self.g.depth:
@@ -130,9 +139,9 @@
             if 2 <= t <= self.g.depth + 1:
                 self.cross(r, 'c', t - 2)
     def steps(self):
-        return self.g.depth + len(self.rest)
+        return self.g.depth + len(self.order) - 1
     def arrive(self):
-        r = self.rest
+        r = 'yx' if self.early else self.rest
         sets = ['', r[0]] + ([r[1], r] if len(r) > 1 else [])
         for f in sets:
             def go(k, f=f):
@@ -147,39 +156,61 @@
                       else jnp.logical_and(self.z > 0, k >= self.z))
                 @pl.when(ok)
                 def _():
-                    self.wait(self.at('', k), self.zsend.at[n, k])
+                    for f in ('', 'y') if self.early else ('',):
+                        self.wait(self.at(f, k), self.zsend.at[n, k + (self.g.depth if f else 0)])
         each(self.g.depth, sent)
         p = self.g.depth
-        n = p + (2 * p + 4 * p if len(self.rest) > 1 else 2 * p)
+        n = 6 * p + 1 if self.early else p + (2 * p + 4 * p if len(self.rest) > 1 else 2 * p)
         v = self.rows(0, n)
         pltpu.make_async_copy(v, v, self.send).wait()
 
-PLAN = ("q0", "q1", "q2", "q3", "w0", "q4", "w1", "q5", "qa", "k0", "k1", "w2", "k2", "w3", "k3", "w4", "k4", "w5")
-
-def fetch_kernel(grid, scale, *refs):
-    x, w_qkv, vec, w_bias, w_out, w_in, w_back = refs[:7]
-    qkv_all, vec_all, bias_all, out_all, in_all, back_all, key_all, value_all, query = refs[7:16]
-    key, value = refs[16:18]
-    sems = refs[18:]
+WAYS = ("yzx", "zyx")
+PLAN = ("q0", "q1", "q2", "q3", "w0", "q4", "w1", "q5", "qa", "k0", "qq", "k1", "w2", "k2", "w3", "k3", "w4", "k4", "ka", "p0", "p1", "w5", "wa")
+
+def fetch_kernel(grid, size, *refs):
+    length, x, w_qkv, vec, w_bias, w_out, w_in, w_back = refs[:8]
+    qkv_all, vec_all, bias_all, out_all, in_all, back_all, key_all, value_all, query, attended, lse = refs[8:19]
+    key, value, k_slots, v_slots, kv_sem = refs[19:24]
+    sems = refs[24:]
     greet(grid, True)
+    pair, pairs = 2 * size, x.shape[1] // (2 * size)
+    def pull(p):
+        at = pl.multiple_of(p * pair, pair)
+        return [pltpu.make_async_copy(src.at[:, pl.ds(at, pair)], slots.at[lax.rem(p, 2)], kv_sem.at[n, lax.rem(p, 2)])
+                for n, (src, slots) in enumerate(((key_all, k_slots), (value_all, v_slots)))]
+    def attention(first):
+        def one(j, _):
+            p = first + j
+            slot = lax.rem(p, 2)
+            @pl.when(p + 1 < pairs)
+            def _():
+                for copy in pull(p + 1): copy.start()
+            for copy in pull(p): copy.wait()
+            at = pl.ds(pl.multiple_of(p * pair, pair), pair)
+            attended[:, at], lse[p] = forward_math(size, length[0], query[:, at], k_slots[slot], v_slots[slot])
+            return _
+        lax.fori_loop(0, pairs // 2, one, None)
     def job(i, src, dst, order, cols=None):
         return Gather(grid, src, dst, [r.at[i] for r in sems], order, cols)
     width = x.shape[1]
     half = 3 * width // 2
     parts = {
         "q": [job(0, vec, vec_all, "zyx"), job(1, w_qkv, qkv_all, "zyx", pl.ds(0, half)), job(2, w_qkv, qkv_all, "zxy", pl.ds(half, half))],
-        "w": [job(3, w_bias, bias_all, "zyx"), job(4, w_out, out_all, "zyx"), job(5, w_in, in_all, "zyx"), job(6, w_back, back_all, "zyx")],
+        "w": [job(3, w_bias, bias_all, "zyx"), job(4, w_out, out_all, "zyx"), job(5, w_in, in_all, WAYS[0]), job(6, w_back, back_all, WAYS[1])],
         "k": [job(7, key, key_all, "zy"), job(8, value, value_all, "zy")]}
     for word in PLAN:
+        if word == "p0":
+            for copy in pull(0): copy.start()
+        if word[0] == "p":
+            attention(int(word[1]) * (pairs // 2))
+            continue
+        if word == "qq":
+            q = (nn(x[...], qkv_all[:, :width]) + rows[0:1]).astype(jnp.bfloat16)
+            query[...] = q * jnp.asarray(size ** -0.5, jnp.bfloat16)
+            continue
         jobs, t = parts[word[0]], word[1]
         for j in jobs:
             if t == "a": j.arrive()
-            elif t == "s": j.start("xc")
-            elif t == "l": j.line(int(word[2]), "xc")
-            elif t == "y": j.late("y", int(word[2]))
-            elif t == "b": j.cross("y", "xc", int(word[2]))
-            elif t == "x": j.cross("x", "c", int(word[2]))
-            elif t == "z": j.cross("yx", "c", int(word[2]))
             elif t == "0": j.start()
             else: j.step(int(t))
         if word == "qa":
@@ -188,14 +219,10 @@
             rows = nt(pick, vec_all[...])
             key[...] = nn(x[...], qkv_all[:, width:2 * width]).astype(jnp.bfloat16)
             value[...] = (nn(x[...], qkv_all[:, 2 * width:]) + rows[1:2]).astype(jnp.bfloat16)
-    q = (nn(x[...], qkv_all[:, :width]) + rows[0:1]).astype(jnp.bfloat16)
-    query[...] = q * jnp.asarray(scale, jnp.bfloat16)
-    for j in parts["k"] + parts["w"]:
-        j.arrive()
     for j in parts["q"] + parts["k"] + parts["w"]:
         j.leave()
 
-def fetch(grid, x, w_qkv, vec, w_bias, w_out, w_in, w_back, scale):
+def fetch(grid, size, length, x, w_qkv, vec, w_bias, w_out, w_in, w_back):
     devices, bf = grid.seqs * grid.ctx, jnp.bfloat16
     rows, width = x.shape
     S = jax.ShapeDtypeStruct
@@ -205,14 +232,15 @@
     deep = lambda a: S((devices,) + a.shape[1:], bf)
     kv = S((grid.ctx * rows, width), bf)
     return pl.pallas_call(
-        functools.partial(fetch_kernel, grid, scale),
-        out_shape=[flat(w_qkv), flat(vec), deep(w_bias), deep(w_out), deep(w_in), deep(w_back), kv, kv, S((rows, width), bf)],
-        in_specs=[V] * 7,
-        out_specs=[V, V] + [A] * 6 + [V],
-        scratch_shapes=[pltpu.VMEM((rows, width), bf)] * 2 + [D((9,)), D((9, 2, grid.depth)), D((9, devices)), D((9,))],
+        functools.partial(fetch_kernel, grid, size),
+        out_shape=[flat(w_qkv), flat(vec), deep(w_bias), deep(w_out), deep(w_in), deep(w_back), kv, kv, S((rows, width), bf),
+                   S((rows, width), jnp.float32), S((width // (2 * size), 1, 2 * rows), jnp.float32)],
+        in_specs=[pl.BlockSpec(memory_space=pltpu.SMEM)] + [V] * 7,
+        out_specs=[V, V] + [A] * 6 + [V] * 3,
+        scratch_shapes=[pltpu.VMEM((rows, width), bf)] * 2 + [pltpu.VMEM((2, grid.ctx * rows, 2 * size), bf)] * 2 + [D((2, 2)), D((9,)), D((9, 2, 2 * grid.depth)), D((9, devices)), D((9,))],
         compiler_params=pltpu.CompilerParams(collective_id=0, has_side_effects=True, vmem_limit_bytes=60 * 2**20),
         name="fetch",
-    )(x, w_qkv, vec, w_bias, w_out, w_in, w_back)
+    )(length, x, w_qkv, vec, w_bias, w_out, w_in, w_back)
 from jax.sharding import PartitionSpec as P
 
 def f32(x):
@@ -258,8 +286,8 @@
             each(self.g.depth, go)
     def loaded(self):
         pltpu.make_async_copy(self.mine, self.mine, self.local).wait()
-    def start(self):
-        for f in self.combos():
+    def start(self, which=slice(None)):
+        for f in self.combos()[which]:
             def go(z, side, f=f):
                 k = self.idx(f, z)
                 self.push(self.src.at[self.at(self.flips(f) + 'c', z)], self.bufc.at[k], self.rc.at[k], 'c')
@@ -365,6 +393,14 @@
 
 MASKED = -1e30
 
+def forward_math(half, length, q, k, v):
+    s = nt(pair_stack(q, half), k)
+    s = jnp.where(lax.broadcasted_iota(jnp.int32, (1, s.shape[1]), 1) < length, s, MASKED)
+    top = jnp.max(s, axis=1, keepdims=True)
+    p = jnp.exp(s - top)
+    total = jnp.sum(p, axis=1, keepdims=True)
+    return pair_join(nn(p.astype(jnp.bfloat16), v) / total, half), as_row(top + jnp.log(total))
+
 def forward_kernel(half, tiles, len_ref, q_ref, k_ref, v_ref, o_ref, lse_ref, top_ref, sum_ref, acc_ref):
     t = pl.program_id(1)
     q2 = pair_stack(q_ref[...], half)
@@ -450,7 +486,7 @@
         out_shape=[jax.ShapeDtypeStruct((rows, width), jnp.bfloat16)] + [jax.ShapeDtypeStruct((total, width), jnp.bfloat16)] * 2 + [jax.ShapeDtypeStruct((pairs, 1, wide), jnp.float32)],
         name="attend_back",
     )(length, q, k, v, g, o, lse)
-ORDER = ("ds", "pA", "ld", "d1,*", "As", "A1,*", "pB", "Bs", "B1,*", "d2,*", "e", "A4,*", "B4,d3,*", "g", "qs", "q1,*", "q2,*", "d4,*", "i", "q3,*", "q4,*")
+ORDER = ("du", "pA", "ld", "d1,*", "As", "A1,*", "dv", "pB", "Bs", "B1,*", "d2,*", "e", "A4,*", "B4,d3,*", "g", "qs", "q1,*", "q2,*", "d4,*", "i", "q3,*", "q4,*")
 
 def settle_kernel(grid, size, *refs):
     length, key_all, value_all, g_out, g_in, g_back, w_qkv, q, g, o, lse, x, base, g_bias, g_vec = refs[:15]
@@ -526,9 +562,10 @@
              "ld": lambda: [job.loaded() for job in big]}
     def step(word, d):
         for job in jobs[word[0]]:
-            if word[1] == "s":
+            if word[1] in "su":
                 if job.mine is not None: job.load()
-                job.start()
+                job.start(slice(None, None if word[1] == "s" else 1))
+            elif word[1] == "v": job.start(slice(1, None))
             elif word[1] == "1": job.stage1(job.combos()[0], d)
             elif word[1] == "2": job.stage1((1, 0), d)
             elif word[1] == "3": job.stage2(d)
@@ -545,7 +582,7 @@
             for word in words[:-1]: step(word, None)
         else:
             for word in words: step(word, None)
-    for group in [n for n in "ABdq" if n + "s" in ORDER]:
+    for group in "ABdq":
         for job in jobs[group]: job.finish()
 
 def settle(grid, size, length, key_all, value_all, g_out, g_in, g_back, w_qkv, q, g, o, lse, x, base, g_bias, g_vec):
@@ -699,8 +736,8 @@
     if whole:
         vec_block = jnp.pad(vectors, ((0, 0), (0, 120)))
         bias_block = jnp.pad(ffn_bias[None], ((0, 7), (0, 128 - part_ff)))[None]
-        qkv_full, vec_all, bias_all, out_all, in_all, back_all, key_all, value_all, query_scaled = fetch(
-            grid, rows_in, w_qkv, vec_block, bias_block, w_out[None], w_in[None], w_back[None], scale)
+        qkv_full, vec_all, bias_all, out_all, in_all, back_all, key_all, value_all, query_scaled, attended_f, lse = fetch(
+            grid, width // HEADS, lengths, rows_in, w_qkv, vec_block, bias_block, w_out[None], w_in[None], w_back[None])
         out_full, in_full, back_full = out_all.reshape(width, width), in_all.reshape(width, hidden_size), back_all.reshape(hidden_size, width)
     else:
         everywhere = lambda a: lax.all_gather(a, ("seq", "ctx"), axis=0, tiled=True)
@@ -713,8 +750,6 @@
         value = (projected[:, 2 * width:] + vec[1]).astype(bf)
         key_all, value_all = (lax.all_gather(a, "ctx", axis=0, tiled=True) for a in (key, value))
 
-    tile = min(slots, 2048)
-    attended_f, lse = attend(query_scaled, key_all, value_all, lengths, HEADS, tile)
     if whole:
         g_out, g_in, g_back, result, grad_attended, base, g_bias, g_vec = layer(
             grid, lengths, out_full, in_full, back_full, attended_f, rows_in, cotangent[0], vec_all, bias_all)
@@ -724,6 +759,8 @@
             (grad_inputs, d_qkv, d_out, d_in, d_back, d_vec, d_bias),
             ((1, rows, width), (part, 3 * width), (part, width), (part, hidden_size), (part_ff, width), (part, 8), (1, part_ff)))
         return (result[None], grad_inputs, d_qkv, d_out, d_in, d_back, d_vec, d_bias[0])
+    tile = min(slots, 2048)
+    attended_f, lse = attend(query_scaled, key_all, value_all, lengths, HEADS, tile)
     attended = attended_f.astype(bf)
     branch = jnp.dot(attended, out_full, preferred_element_type=f4) + vec[2]
     norm_one, r_one = normalize(rows_in.astype(f4) + branch)

time: 232 us -> 226 us (0.974)
  Pallas kernels: 226 us -> 220 us
    pallas_call x1, Pallas kernels: 106 us -> 101 us  [settle(): pl.pallas_call(functools.partial(settle_kernel, grid, size), out_shape=[S...]
    pallas_call x2 -> x1, Pallas kernels: 101 us -> 99.1 us  [fetch(): pl.pallas_call(functools.partial(fetch_kernel, grid, size), out_shape=[fl...]
where the time goes in v5:
time: 226 us; the launch traced here: 225 us
  Pallas kernels  220 us (97%)
  local copies, waits for them, and re-layouts  3.97 us (2%)
    pallas_call x1, Pallas kernels, settle(): pl.pallas_call(functools.partial(settle_kernel, grid, size), out_shape=[S...  101 us
    pallas_call x1, Pallas kernels, fetch(): pl.pallas_call(functools.partial(fetch_kernel, grid, size), out_shape=[fl...  99.1 us
    pallas_call x1, Pallas kernels, layer(): pl.pallas_call(functools.partial(layer_kernel, grid), out_shape=[S(g, bf)...  17.4 us

profile of v5, /device:TPU:0, one launch (start us, length us, event | category | flops | bytes accessed | tf_op | source)
XLA Modules:
  0.0 225.4 jit_solution(8588049035293493553)
XLA Ops:
  1.3 1.2 pad_bitcast_fusion.refs_4_
  2.5 0.8 copy.17
  3.3 0.6 pad.8.refs_3_
  3.9 99.1 %fetch.1 = (bf16[768,2304]{1,0:T(8,128)(2,1)}, bf16[768,128]{1,0:T(8,128)(2,1)}, bf16[32,8,128]{2,1,0:T(8,128)(2,1)}, bf16[32,24,768]{2,1,0:T(8,128)(2,1)}, bf16...) custom-call(s32[1]{0:T(128)S(6)} %copy.19.refs_0_.length, ...), custom_call_target="tpu_custom_call" | custom-call | tf_op jit(solution)/shard_map/fetch/pallas_call | solution.py:234
  103.0 17.4 %layer.1 = (bf16[32,24,768]{2,1,0:T(8,128)(2,1)}, bf16[32,24,3072]{2,1,0:T(8,128)(2,1)}, bf16[32,96,768]{2,1,0:T(8,128)(2,1)}, bf16[128,768]{1,0:T(8,128)(2,1)},...) custom-call(s32[1]{0:T(128)S(6)} %copy.19.refs_0_.length, ...), custom_call_target="tpu_custom_call" | custom-call | tf_op jit(solution)/shard_map/layer/pallas_call | solution.py:702
  120.4 101.3 %settle.1 = (f32[1,24,2304]{2,1,0:T(8,128)}, f32[1,24,768]{2,1,0:T(8,128)}, f32[1,24,3072]{2,1,0:T(8,128)}, f32[1,96,768]{2,1,0:T(8,128)}, f32[1,8,128]{2,1,0:T(...) custom-call(s32[1]{0:T(128)S(6)} %copy.19.refs_0_.length, bf16[2048,768]{1,0:T(8,128)(2,1)} %get-tuple-element.48.refs_1_, ...), custom_call_target="tpu_custom_call" | custom-call | tf_op jit(solution)/shard_map/settle/pallas_call | solution.py:603
  221.7 2.4 %deliver.1 = (f32[1,128,768]{2,1,0:T(8,128)}, f32[24,2304]{1,0:T(8,128)}, f32[24,768]{1,0:T(8,128)}, f32[24,3072]{1,0:T(8,128)}, f32[96,768]{1,0:T(8,128)}, /*index=5*/f32[24,8]{1,0:T(8,128)}, f32[1,96]{1,0:T(1,128)}) custom-call(f32[128,768]{1,0:T(8,128)} %get-tuple-element.60.refs_0_, f32[1,24,2304]{2,1,0:T(8,128)} %get-tuple-element.61.refs_1_, ...), custom_call_target="tpu_custom_call" | custom-call | tf_op jit(solution)/shard_map/deliver/pallas_call | solution.py:719
  224.0 1.4 copy.18

commit v6 on v5

--- a/solution.py
+++ b/solution.py
@@ -168,10 +168,16 @@
 PLAN = ("q0", "q1", "q2", "q3", "w0", "q4", "w1", "q5", "qa", "k0", "qq", "k1", "w2", "k2", "w3", "k3", "w4", "k4", "ka", "p0", "p1", "w5", "wa")
 
 def fetch_kernel(grid, size, *refs):
-    length, x, w_qkv, vec, w_bias, w_out, w_in, w_back = refs[:8]
+    length, x, w_qkv, vec_rows, bias_row, w_out, w_in, w_back = refs[:8]
     qkv_all, vec_all, bias_all, out_all, in_all, back_all, key_all, value_all, query, attended, lse = refs[8:19]
-    key, value, k_slots, v_slots, kv_sem = refs[19:24]
-    sems = refs[24:]
+    key, value, k_slots, v_slots, vec, w_bias, room, kv_sem = refs[19:27]
+    sems = refs[27:]
+    part, part_ff = vec.shape[0], bias_row.shape[1]
+    room[...] = jnp.zeros_like(room)
+    room[0:8, 0:part] = f32(vec_rows[...])
+    vec[...] = jnp.transpose(room[...])[0:part].astype(vec.dtype)
+    room[0:1, 0:part_ff] = f32(bias_row[...])
+    w_bias[0] = room[0:8, :].astype(w_bias.dtype)
     greet(grid, True)
     pair, pairs = 2 * size, x.shape[1] // (2 * size)
     def pull(p):
@@ -222,7 +228,7 @@
     for j in parts["q"] + parts["k"] + parts["w"]:
         j.leave()
 
-def fetch(grid, size, length, x, w_qkv, vec, w_bias, w_out, w_in, w_back):
+def fetch(grid, size, length, x, w_qkv, vec_rows, bias_row, w_out, w_in, w_back):
     devices, bf = grid.seqs * grid.ctx, jnp.bfloat16
     rows, width = x.shape
     S = jax.ShapeDtypeStruct
@@ -233,14 +239,15 @@
     kv = S((grid.ctx * rows, width), bf)
     return pl.pallas_call(
         functools.partial(fetch_kernel, grid, size),
-        out_shape=[flat(w_qkv), flat(vec), deep(w_bias), deep(w_out), deep(w_in), deep(w_back), kv, kv, S((rows, width), bf),
+        out_shape=[flat(w_qkv), S((width, 128), bf), S((devices, 8, 128), bf), deep(w_out), deep(w_in), deep(w_back), kv, kv, S((rows, width), bf),
                    S((rows, width), jnp.float32), S((width // (2 * size), 1, 2 * rows), jnp.float32)],
         in_specs=[pl.BlockSpec(memory_space=pltpu.SMEM)] + [V] * 7,
         out_specs=[V, V] + [A] * 6 + [V] * 3,
-        scratch_shapes=[pltpu.VMEM((rows, width), bf)] * 2 + [pltpu.VMEM((2, grid.ctx * rows, 2 * size), bf)] * 2 + [D((2, 2)), D((9,)), D((9, 2, 2 * grid.depth)), D((9, devices)), D((9,))],
+        scratch_shapes=[pltpu.VMEM((rows, width), bf)] * 2 + [pltpu.VMEM((2, grid.ctx * rows, 2 * size), bf)] * 2
+                       + [pltpu.VMEM((width // devices, 128), bf), pltpu.VMEM((1, 8, 128), bf), pltpu.VMEM((128, 128), jnp.float32)] + [D((2, 2)), D((9,)), D((9, 2, 2 * grid.depth)), D((9, devices)), D((9,))],
         compiler_params=pltpu.CompilerParams(collective_id=0, has_side_effects=True, vmem_limit_bytes=60 * 2**20),
         name="fetch",
-    )(length, x, w_qkv, vec, w_bias, w_out, w_in, w_back)
+    )(length, x, w_qkv, vec_rows, bias_row, w_out, w_in, w_back)
 from jax.sharding import PartitionSpec as P
 
 def f32(x):
@@ -710,8 +717,11 @@
 
 def deliver_kernel(*refs):
     n = len(refs) // 2
-    for src, dst in zip(refs[:n], refs[n:]):
-        if len(dst.shape) == 3: dst[0] = src[...]
+    for k, (src, dst) in enumerate(zip(refs[:n], refs[n:])):
+        if k == 0:
+            tall = jnp.concatenate((src[0], jnp.zeros((128 - src.shape[1], 128), jnp.float32)), axis=0)
+            dst[...] = jnp.transpose(tall)[:dst.shape[0], :dst.shape[1]]
+        elif len(dst.shape) == 3: dst[0] = src[...]
         else: dst[...] = src[0, :dst.shape[0], :dst.shape[1]]
 
 def deliver(arrays, shapes):
@@ -734,10 +744,8 @@
     half = 3 * width // 2
     whole = grid.depth <= 4 and part % 8 == 0 and part_ff <= 128
     if whole:
-        vec_block = jnp.pad(vectors, ((0, 0), (0, 120)))
-        bias_block = jnp.pad(ffn_bias[None], ((0, 7), (0, 128 - part_ff)))[None]
         qkv_full, vec_all, bias_all, out_all, in_all, back_all, key_all, value_all, query_scaled, attended_f, lse = fetch(
-            grid, width // HEADS, lengths, rows_in, w_qkv, vec_block, bias_block, w_out[None], w_in[None], w_back[None])
+            grid, width // HEADS, lengths, rows_in, w_qkv, vectors.T, ffn_bias[None], w_out[None], w_in[None], w_back[None])
         out_full, in_full, back_full = out_all.reshape(width, width), in_all.reshape(width, hidden_size), back_all.reshape(hidden_size, width)
     else:
         everywhere = lambda a: lax.all_gather(a, ("seq", "ctx"), axis=0, tiled=True)
@@ -755,10 +763,10 @@
             grid, lengths, out_full, in_full, back_full, attended_f, rows_in, cotangent[0], vec_all, bias_all)
         d_qkv, d_out, d_in, d_back, d_bias, d_vec, grad_inputs = settle(
             grid, width // HEADS, lengths, key_all, value_all, g_out, g_in, g_back, qkv_full, query_scaled, grad_attended, attended_f, lse, rows_in, base, g_bias, g_vec)
-        grad_inputs, d_qkv, d_out, d_in, d_back, d_vec, d_bias = deliver(
-            (grad_inputs, d_qkv, d_out, d_in, d_back, d_vec, d_bias),
-            ((1, rows, width), (part, 3 * width), (part, width), (part, hidden_size), (part_ff, width), (part, 8), (1, part_ff)))
-        return (result[None], grad_inputs, d_qkv, d_out, d_in, d_back, d_vec, d_bias[0])
+        d_vec, grad_inputs, d_qkv, d_out, d_in, d_back, d_bias = deliver(
+            (d_vec, grad_inputs, d_qkv, d_out, d_in, d_back, d_bias),
+            ((8, part), (1, rows, width), (part, 3 * width), (part, width), (part, hidden_size), (part_ff, width), (1, part_ff)))
+        return (result[None], grad_inputs, d_qkv, d_out, d_in, d_back, d_vec.T, d_bias[0])
     tile = min(slots, 2048)
     attended_f, lse = attend(query_scaled, key_all, value_all, lengths, HEADS, tile)
     attended = attended_f.astype(bf)

time: 226 us -> 222 us (0.982)
  local copies, waits for them, and re-layouts: 3.97 us -> 0 us
where the time goes in v6:
time: 222 us
  Pallas kernels  220 us (99%)
    pallas_call x1, Pallas kernels, settle(): pl.pallas_call(functools.partial(settle_kernel, grid, size), out_shape=[S...  101 us
    pallas_call x1, Pallas kernels, fetch(): pl.pallas_call(functools.partial(fetch_kernel, grid, size), out_shape=[fl...  99.2 us
    pallas_call x1, Pallas kernels, layer(): pl.pallas_call(functools.partial(layer_kernel, grid), out_shape=[S(g, bf)...  17.4 us

profile of v6, /device:TPU:0, one launch (start us, length us, event | category | flops | bytes accessed | tf_op | source)
XLA Modules:
  0.0 221.5 jit_solution(2495618512520287705)
XLA Ops:
  1.3 99.2 %fetch.1 = (bf16[768,2304]{1,0:T(8,128)(2,1)}, bf16[768,128]{1,0:T(8,128)(2,1)}, bf16[32,8,128]{2,1,0:T(8,128)(2,1)}, bf16[32,24,768]{2,1,0:T(8,128)(2,1)}, bf16...) custom-call(s32[1]{0:T(128)S(6)} %copy.17.refs_0_.length, ...), custom_call_target="tpu_custom_call" | custom-call | tf_op jit(solution)/shard_map/fetch/pallas_call | solution.py:240
  100.5 17.4 %layer.1 = (bf16[32,24,768]{2,1,0:T(8,128)(2,1)}, bf16[32,24,3072]{2,1,0:T(8,128)(2,1)}, bf16[32,96,768]{2,1,0:T(8,128)(2,1)}, bf16[128,768]{1,0:T(8,128)(2,1)},...) custom-call(s32[1]{0:T(128)S(6)} %copy.17.refs_0_.length, ...), custom_call_target="tpu_custom_call" | custom-call | tf_op jit(solution)/shard_map/layer/pallas_call | solution.py:709
  117.9 101.2 %settle.1 = (f32[1,24,2304]{2,1,0:T(8,128)}, f32[1,24,768]{2,1,0:T(8,128)}, f32[1,24,3072]{2,1,0:T(8,128)}, f32[1,96,768]{2,1,0:T(8,128)}, f32[1,8,128]{2,1,0:T(...) custom-call(s32[1]{0:T(128)S(6)} %copy.17.refs_0_.length, bf16[2048,768]{1,0:T(8,128)(2,1)} %get-tuple-element.48.refs_1_, ...), custom_call_target="tpu_custom_call" | custom-call | tf_op jit(solution)/shard_map/settle/pallas_call | solution.py:610
  219.2 2.4 %deliver.1 = (f32[8,24]{1,0:T(8,128)}, f32[1,128,768]{2,1,0:T(8,128)}, f32[24,2304]{1,0:T(8,128)}, f32[24,768]{1,0:T(8,128)}, f32[24,3072]{1,0:T(8,128)}, /*index=5*/f32[96,768]{1,0:T(8,128)}, f32[1,96]{1,0:T(1,128)}) custom-call(f32[1,24,128]{2,1,0:T(8,128)} %get-tuple-element.60.refs_0_, f32[128,768]{1,0:T(8,128)} %get-tuple-element.61.refs_1_, ...), custom_call_target="tpu_custom_call" | custom-call | tf_op jit(solution)/shard_map/deliver/pallas_call | solution.py:729

commit v7 on v6

--- a/solution.py
+++ b/solution.py
@@ -165,7 +165,7 @@
         pltpu.make_async_copy(v, v, self.send).wait()
 
 WAYS = ("yzx", "zyx")
-PLAN = ("q0", "q1", "q2", "q3", "w0", "q4", "w1", "q5", "qa", "k0", "qq", "k1", "w2", "k2", "w3", "k3", "w4", "k4", "ka", "p0", "p1", "w5", "wa")
+PLAN = ("q0", "q1", "q2", "q3", "w0", "q4", "w1", "q5", "qa", "k0", "qq", "k1", "l0", "w2", "k2", "l1", "w3", "k3", "l2", "k4", "w4", "ka", "l3", "p0", "l4", "la", "p1", "w5", "wa")
 
 def fetch_kernel(grid, size, *refs):
     length, x, w_qkv, vec_rows, bias_row, w_out, w_in, w_back = refs[:8]
@@ -188,7 +188,7 @@
         def one(j, _):
             p = first + j
             slot = lax.rem(p, 2)
-            @pl.when(p + 1 < pairs)
+            @pl.when(j + 1 < pairs // 2)
             def _():
                 for copy in pull(p + 1): copy.start()
             for copy in pull(p): copy.wait()
@@ -203,12 +203,13 @@
     parts = {
         "q": [job(0, vec, vec_all, "zyx"), job(1, w_qkv, qkv_all, "zyx", pl.ds(0, half)), job(2, w_qkv, qkv_all, "zxy", pl.ds(half, half))],
         "w": [job(3, w_bias, bias_all, "zyx"), job(4, w_out, out_all, "zyx"), job(5, w_in, in_all, WAYS[0]), job(6, w_back, back_all, WAYS[1])],
-        "k": [job(7, key, key_all, "zy"), job(8, value, value_all, "zy")]}
+        "k": [job(7, key, key_all, "zy", pl.ds(0, width // 2)), job(8, value, value_all, "zy", pl.ds(0, width // 2))],
+        "l": [job(9, key, key_all, "zy", pl.ds(width // 2, width // 2)), job(10, value, value_all, "zy", pl.ds(width // 2, width // 2))]}
     for word in PLAN:
-        if word == "p0":
-            for copy in pull(0): copy.start()
         if word[0] == "p":
-            attention(int(word[1]) * (pairs // 2))
+            first = int(word[1]) * (pairs // 2)
+            for copy in pull(first): copy.start()
+            attention(first)
             continue
         if word == "qq":
             q = (nn(x[...], qkv_all[:, :width]) + rows[0:1]).astype(jnp.bfloat16)
@@ -225,7 +226,7 @@
             rows = nt(pick, vec_all[...])
             key[...] = nn(x[...], qkv_all[:, width:2 * width]).astype(jnp.bfloat16)
             value[...] = (nn(x[...], qkv_all[:, 2 * width:]) + rows[1:2]).astype(jnp.bfloat16)
-    for j in parts["q"] + parts["k"] + parts["w"]:
+    for j in parts["q"] + parts["k"] + parts["l"] + parts["w"]:
         j.leave()
 
 def fetch(grid, size, length, x, w_qkv, vec_rows, bias_row, w_out, w_in, w_back):
@@ -244,7 +245,7 @@
         in_specs=[pl.BlockSpec(memory_space=pltpu.SMEM)] + [V] * 7,
         out_specs=[V, V] + [A] * 6 + [V] * 3,
         scratch_shapes=[pltpu.VMEM((rows, width), bf)] * 2 + [pltpu.VMEM((2, grid.ctx * rows, 2 * size), bf)] * 2
-                       + [pltpu.VMEM((width // devices, 128), bf), pltpu.VMEM((1, 8, 128), bf), pltpu.VMEM((128, 128), jnp.float32)] + [D((2, 2)), D((9,)), D((9, 2, 2 * grid.depth)), D((9, devices)), D((9,))],
+                       + [pltpu.VMEM((width // devices, 128), bf), pltpu.VMEM((1, 8, 128), bf), pltpu.VMEM((128, 128), jnp.float32)] + [D((2, 2)), D((11,)), D((11, 2, 2 * grid.depth)), D((11, devices)), D((11,))],
         compiler_params=pltpu.CompilerParams(collective_id=0, has_side_effects=True, vmem_limit_bytes=60 * 2**20),
         name="fetch",
     )(length, x, w_qkv, vec_rows, bias_row, w_out, w_in, w_back)
@@ -514,7 +515,7 @@
     part_of = lambda ref, n: ref.at[:, :, pl.ds(n * third, third)]
     specs = [("A", vA, part_of(own_value, 0), "zy"), ("A", kA, part_of(own_key, 0), "zy"), ("B", vB, part_of(own_value, 1), "zy"), ("B", kB, part_of(own_key, 1), "zy"),
              ("d", g_back, d_back, "zyx"), ("d", g_in, d_in, "zyx"), ("d", g_out, d_out, "zyx"), ("d", g_bias, d_bias, "zyx"),
-             ("q", vec_src, d_vec, "zyx"), ("q", w_query, cut(0), "zyx"), ("q", w_key, cut(1), "zyx"), ("q", w_value, cut(2), "zxy")]
+             ("q", vec_src, d_vec, "zyx"), ("q", w_query, cut(0), "zyx"), ("q", w_key, cut(1), "zyx"), ("q", w_value, cut(2), "zyx")]
     jobs = {"A": [], "B": [], "d": [], "q": []}
     for n, (group, src, out, order) in enumerate(specs):
         r = bufs[10 * n:10 * n + 10]

time: 222 us -> 223 us (level)
  no operation moved by 1% of the time
where the time goes in v7:
time: 223 us
  Pallas kernels  222 us (100%)
    pallas_call x1, Pallas kernels, settle(): pl.pallas_call(functools.partial(settle_kernel, grid, size), out_shape=[S...  103 us
    pallas_call x1, Pallas kernels, fetch(): pl.pallas_call(functools.partial(fetch_kernel, grid, size), out_shape=[fl...  98.5 us
    pallas_call x1, Pallas kernels, layer(): pl.pallas_call(functools.partial(layer_kernel, grid), out_shape=[S(g, bf)...  17.4 us

profile of v7, /device:TPU:0, one launch (start us, length us, event | category | flops | bytes accessed | tf_op | source)
XLA Modules:
  0.0 223.1 jit_solution(12718867365437216059)
XLA Ops:
  1.3 98.5 %fetch.1 = (bf16[768,2304]{1,0:T(8,128)(2,1)}, bf16[768,128]{1,0:T(8,128)(2,1)}, bf16[32,8,128]{2,1,0:T(8,128)(2,1)}, bf16[32,24,768]{2,1,0:T(8,128)(2,1)}, bf16...) custom-call(s32[1]{0:T(128)S(6)} %copy.17.refs_0_.length, ...), custom_call_target="tpu_custom_call" | custom-call | tf_op jit(solution)/shard_map/fetch/pallas_call | solution.py:241
  99.8 17.4 %layer.1 = (bf16[32,24,768]{2,1,0:T(8,128)(2,1)}, bf16[32,24,3072]{2,1,0:T(8,128)(2,1)}, bf16[32,96,768]{2,1,0:T(8,128)(2,1)}, bf16[128,768]{1,0:T(8,128)(2,1)},...) custom-call(s32[1]{0:T(128)S(6)} %copy.17.refs_0_.length, ...), custom_call_target="tpu_custom_call" | custom-call | tf_op jit(solution)/shard_map/layer/pallas_call | solution.py:710
  117.2 103.5 %settle.1 = (f32[1,24,2304]{2,1,0:T(8,128)}, f32[1,24,768]{2,1,0:T(8,128)}, f32[1,24,3072]{2,1,0:T(8,128)}, f32[1,96,768]{2,1,0:T(8,128)}, f32[1,8,128]{2,1,0:T(...) custom-call(s32[1]{0:T(128)S(6)} %copy.17.refs_0_.length, bf16[2048,768]{1,0:T(8,128)(2,1)} %get-tuple-element.48.refs_1_, ...), custom_call_target="tpu_custom_call" | custom-call | tf_op jit(solution)/shard_map/settle/pallas_call | solution.py:611
  220.7 2.4 %deliver.1 = (f32[8,24]{1,0:T(8,128)}, f32[1,128,768]{2,1,0:T(8,128)}, f32[24,2304]{1,0:T(8,128)}, f32[24,768]{1,0:T(8,128)}, f32[24,3072]{1,0:T(8,128)}, /*index=5*/f32[96,768]{1,0:T(8,128)}, f32[1,96]{1,0:T(1,128)}) custom-call(f32[1,24,128]{2,1,0:T(8,128)} %get-tuple-element.60.refs_0_, f32[128,768]{1,0:T(8,128)} %get-tuple-element.61.refs_1_, ...), custom_call_target="tpu_custom_call" | custom-call | tf_op jit(solution)/shard_map/deliver/pallas_call | solution.py:730
